TPU v7x, 32 devices: a whole 2x2x4 slice. The times are simulated.
32 devices in a mesh: gx: 2 (over y), gy: 4 (over z), gz: 4 (over x, core).
Axes of the slice: x: 2, y: 2, z: 4, core: 2. Of those that a mesh axis runs over, the one named last changes fastest.
Arguments:
- positions: float32 [4, 4, 4, 3, 32], P('gx', 'gy', 'gz'), may hold values from 0 to 5, as said below
- counts: int32 [4, 4, 4], P('gx', 'gy', 'gz'), may hold values from 1 to 32, as said below
- scalars: bfloat16 [4, 4, 4, 32, 128], P('gx', 'gy', 'gz'), may hold values from -6 to 6
- vectors: bfloat16 [4, 4, 4, 32, 3, 128], P('gx', 'gy', 'gz'), may hold values from -6 to 6
- radial_in: bfloat16 [2, 8, 64], replicated, may hold values from -2 to 2
- radial_bias: float32 [2, 64], replicated, may hold values from -3 to 3
- radial_out: bfloat16 [2, 64, 512], replicated, may hold values from -0.75 to 0.75
- atom_in: bfloat16 [2, 128, 128], replicated, may hold values from -0.5 to 0.5
- atom_bias: float32 [2, 128], replicated, may hold values from -3 to 3
- atom_out: bfloat16 [2, 128, 512], replicated, may hold values from -0.5 to 0.5
- readout_in: bfloat16 [128, 64], replicated, may hold values from -0.5 to 0.5
- readout_out: float32 [64], replicated, may hold values from -0.75 to 0.75
Outputs:
- scalars_out: bfloat16 [4, 4, 4, 32, 128], P('gx', 'gy', 'gz')
- vectors_out: bfloat16 [4, 4, 4, 32, 3, 128], P('gx', 'gy', 'gz')
- energy: float32 [1], replicated
Inputs may be any that keep to these rules, and one draw needn't show every extreme that they name: `counts`: some cell of every draw holds 32 atoms and some other cell one atom. `positions`: the slots of a cell sit on distinct sites of a jittered lattice, so that any two slots, also of neighbouring cells, lie at least 0.5 apart.
All inputs are finite; a program needn't handle non-finite values.
Results may differ from a plain program's by a relative error of at most 0.0075.
Values may be sent and summed in bfloat16 or wider, within the bound.
A program may use at most 64 MiB of HBM per device.

v0:
```python
import functools
import math

import jax
import jax.numpy as jnp
from jax import lax
from jax.experimental import pallas as pl
from jax.experimental.pallas import tpu as pltpu
from jax.sharding import PartitionSpec as P

cutoff = 5.0
message_scale = 0.5
group = 8
chunk = 256


MESH = pl.DeviceIdType.MESH
sides = (("gy", 1), ("gx", 0), ("gz", 2))
other_sides = (("gy", 1), ("gz", 2), ("gx", 0))


def ring(axis):
    me = lax.axis_index(axis)
    count = lax.axis_size(axis)
    return lax.rem(me + 1, count), lax.rem(me + count - 1, count)


def prepare(ground, radial_in, radial_bias, places, counts, radial_block, bias_wide):
    wide, deep, tall = ground.shape[:3]
    slots = places.shape[1]
    layers, basis_count, hidden_width = radial_in.shape
    for x in range(wide):
        for y in range(deep):
            for z in range(tall):
                index = (x * deep + y) * tall + z
                tile = ground[x, y, z, 0]
                places[index, :, :8] = tile.T[:slots, :]
                counts[index : index + 1, :] = tile[3:4, :].astype(jnp.int32)
    box = (group, hidden_width, group * basis_count)
    owner = lax.div(lax.broadcasted_iota(jnp.int32, box, 2), basis_count)
    match = owner == lax.broadcasted_iota(jnp.int32, box, 0)
    for layer in range(layers):
        small = 0.5 * radial_in[layer].astype(jnp.float32)
        tall_form = jnp.concatenate([small] * group, axis=0)
        wide_form = jnp.concatenate([tall_form] * (128 // hidden_width), axis=1).T[:hidden_width]
        spread = jnp.where(match, jnp.broadcast_to(wide_form[None], box), 0.0)
        radial_block[layer] = spread.reshape(radial_block.shape[1:]).astype(jnp.bfloat16)
        bias = 0.5 * radial_bias[layer : layer + 1, :]
        bias = jnp.concatenate([bias] * (128 // hidden_width), axis=1)
        bias_wide[layer] = jnp.broadcast_to(bias, (chunk, 128)).T[:hidden_width]


def halo_kernel(first, *refs):
    if first:
        blocks, (radial_in, radial_bias) = refs[:3], refs[3:5]
        made = refs[7:11]
        ground, local_sem, send_sem, recv_sem = refs[11:]
        pads = refs[5:7] + (ground,)
    else:
        blocks, pads = refs[:2], refs[2:4]
        local_sem, send_sem, recv_sem = refs[4:]
    dims = blocks[0].shape[:3]
    around = {axis: ring(axis) for axis, _ in sides}
    barrier = pltpu.get_barrier_semaphore()
    for axis, _ in sides:
        for side in around[axis]:
            pl.semaphore_signal(barrier, inc=1, device_id={axis: side}, device_id_type=MESH)
    units = []
    for block, pad in zip(blocks, pads):
        for part in range(block.shape[3]):
            units.append((block, pad, pl.ds(part, 1), sides))
    units = units[::-1]
    units[-1] = units[-1][:3] + (other_sides,)
    center = tuple(pl.ds(1, extent) for extent in dims)
    own = []
    for place, (block, pad) in enumerate(zip(blocks, pads)):
        own.append(pltpu.make_async_copy(block, pad.at[center], local_sem.at[place]))
        own[-1].start()
    pl.semaphore_wait(barrier, 2 * len(sides))
    sent = {}

    def send(stage, number):
        block, pad, part, order = units[number]
        axis, dim = order[stage]
        done = [d for _, d in order[:stage]]
        extent = dims[dim]
        for way, (source, target) in enumerate(((extent, 0), (1, extent + 1))):
            region = [
                pl.ds(0, dims[d] + 2) if d in done else pl.ds(1, dims[d]) for d in range(3)
            ]
            region[dim] = pl.ds(target, 1)
            to = pad.at[tuple(region) + (part,)]
            if stage == 0:
                region = [pl.ds(0, dims[d]) for d in range(3)]
                region[dim] = pl.ds(source - 1, 1)
                come = block.at[tuple(region) + (part,)]
            else:
                region[dim] = pl.ds(source, 1)
                come = pad.at[tuple(region) + (part,)]
            copy = pltpu.make_async_remote_copy(
                src_ref=come,
                dst_ref=to,
                send_sem=send_sem.at[stage, way, number],
                recv_sem=recv_sem.at[stage, way, number],
                device_id={axis: around[axis][way]},
                device_id_type=MESH,
            )
            copy.start()
            sent[stage, way, number] = copy

    for number in range(len(units)):
        send(0, number)
    for copy in own:
        copy.wait()
    for stage in range(1, len(sides) + 1):
        for number in range(len(units)):
            for way in range(2):
                sent[stage - 1, way, number].wait_recv()
            if stage < len(sides):
                send(stage, number)
            elif number == 0 and first:
                prepare(ground, radial_in, radial_bias, *made)
    for copy in sent.values():
        copy.wait_send()


def extended(states, identity, extra=()):
    dims = states[0].shape[:3]
    slots = states[0].shape[4]
    vmem = pl.BlockSpec(memory_space=pltpu.VMEM)
    outer = tuple(d + 2 for d in dims)
    cells = math.prod(outer)
    shapes = [jax.ShapeDtypeStruct(outer + state.shape[3:], state.dtype) for state in states]
    scratch = []
    units = sum(state.shape[3] for state in states)
    if extra:
        layers, basis_count, hidden_width = extra[1].shape
        rows = group * hidden_width
        shapes += [
            jax.ShapeDtypeStruct((cells, slots, 128), jnp.float32),
            jax.ShapeDtypeStruct((cells, 128), jnp.int32),
            jax.ShapeDtypeStruct((layers, rows, group * basis_count), jnp.bfloat16),
            jax.ShapeDtypeStruct((layers, hidden_width, chunk), jnp.float32),
        ]
        scratch = [pltpu.VMEM(outer + extra[0].shape[3:], extra[0].dtype)]
        units += 1
    return pl.pallas_call(
        functools.partial(halo_kernel, bool(extra)),
        out_shape=shapes,
        in_specs=[vmem] * (len(states) + len(extra)),
        out_specs=[vmem] * len(shapes),
        scratch_shapes=scratch
        + [
            pltpu.SemaphoreType.DMA((3,)),
            pltpu.SemaphoreType.DMA((len(sides), 2, units)),
            pltpu.SemaphoreType.DMA((len(sides), 2, units)),
        ],
        compiler_params=pltpu.CompilerParams(collective_id=identity, has_side_effects=True),
        name="halo",
    )(*states, *extra)


def total_kernel(axes, part, out, held, local_sem, send_sem, recv_sem):
    barrier = pltpu.get_barrier_semaphore()
    sizes = [lax.axis_size(axis) for axis in axes]
    places = [lax.axis_index(axis) for axis in axes]
    greeted = 0
    for axis, size, me in zip(axes, sizes, places):
        for step in range(1, size):
            pl.semaphore_signal(
                barrier, inc=1, device_id={axis: lax.rem(me + step, size)}, device_id_type=MESH
            )
            greeted += 1
    own = pltpu.make_async_copy(part, held.at[places[2], places[1], places[0]], local_sem)
    own.start()
    pl.semaphore_wait(barrier, greeted)
    own.wait()
    for stage, (axis, size, me) in enumerate(zip(axes, sizes, places)):
        if stage == 0:
            view = held.at[places[2], places[1], places[0]]
        elif stage == 1:
            view = held.at[places[2], places[1]]
        else:
            view = held.at[places[2]]
        copies = []
        for step in range(1, size):
            copy = pltpu.make_async_remote_copy(
                src_ref=view,
                dst_ref=view,
                send_sem=send_sem.at[stage, step],
                recv_sem=recv_sem.at[stage, step],
                device_id={axis: lax.rem(me + step, size)},
                device_id_type=MESH,
            )
            copy.start()
            copies.append(copy)
        for copy in copies:
            copy.wait()
    out[0] = jnp.sum(held[...]) / (part.shape[0] * part.shape[1])


def summed(part, axes, identity):
    sizes = [lax.axis_size(axis) for axis in axes]
    vmem = pl.BlockSpec(memory_space=pltpu.VMEM)
    return pl.pallas_call(
        functools.partial(total_kernel, axes),
        out_shape=jax.ShapeDtypeStruct((1,), part.dtype),
        in_specs=[vmem],
        out_specs=pl.BlockSpec(memory_space=pltpu.SMEM),
        scratch_shapes=[
            pltpu.VMEM((sizes[2], sizes[1], sizes[0]) + part.shape, part.dtype),
            pltpu.SemaphoreType.DMA,
            pltpu.SemaphoreType.DMA((3, max(sizes))),
            pltpu.SemaphoreType.DMA((3, max(sizes))),
        ],
        compiler_params=pltpu.CompilerParams(collective_id=identity, has_side_effects=True),
        name="total",
    )(part)


def layer_kernel(
    grid_dims,
    max_chunks,
    layer,
    counts,
    places,
    near_scalars,
    near_vectors,
    radial_blocks,
    bias_wide,
    radial_out_all,
    atom_in_all,
    atom_bias_all,
    atom_out_all,
    readout_in,
    readout_out,
    scalars_out,
    vectors_out,
    part_out,
    fresh,
    spots,
    near_place,
    near_state,
    edges,
    plain_table,
    turned_table,
):
    deep, tall = grid_dims
    cell = pl.program_id(0)
    at_x = lax.div(cell, deep * tall)
    at_y = lax.rem(lax.div(cell, tall), deep)
    at_z = lax.rem(cell, tall)
    pad_y, pad_z = deep + 2, tall + 2
    slots, width = near_scalars.shape[2:]
    radial_out = radial_out_all.at[layer]
    atom_out = atom_out_all.at[layer]
    hidden_width = radial_out.shape[0]
    basis_count = radial_blocks.shape[2] // group

    @pl.when(cell == 0)
    def _():
        part_out[...] = jnp.zeros(part_out.shape, part_out.dtype)

    lane = lax.broadcasted_iota(jnp.int32, (slots, width), 1)

    def cell_index(dx, dy, dz):
        return ((at_x + dx) * pad_y + at_y + dy) * pad_z + at_z + dz

    home = cell_index(1, 1, 1)
    total = 0
    own_start = 0
    for dx in range(3):
        for dy in range(3):
            for dz in range(3):
                index = cell_index(dx, dy, dz)
                if (dx, dy, dz) == (1, 1, 1):
                    own_start = total
                shift = jnp.where(
                    lane == 0, float(dx - 1), jnp.where(lane == 1, float(dy - 1), float(dz - 1))
                )
                near_place[pl.ds(total, slots), :] = places[index] + shift * cutoff
                near_state[0, pl.ds(total, slots), :] = near_scalars[index, 0].astype(jnp.float32)
                for part in range(3):
                    near_state[part + 1, pl.ds(total, slots), :] = near_vectors[
                        index, part
                    ].astype(jnp.float32)
                total = total + counts[index, 0]
    blank = jnp.zeros((chunk, width), jnp.float32)
    near_place[pl.ds(total, chunk), :] = blank
    for part in range(4):
        near_state[part, pl.ds(total, chunk), :] = blank
    chunks = lax.div(total + chunk - 1, chunk)

    @pl.loop(0, chunks)
    def _(step):
        rows = pl.ds(pl.multiple_of(step * chunk, chunk), chunk)
        near = near_place[rows, :].T[:8, :]
        mine = places[home]
        col = step * chunk + lax.broadcasted_iota(jnp.int32, (slots, chunk), 1)
        row = lax.broadcasted_iota(jnp.int32, (slots, chunk), 0)
        unused = jnp.logical_or(col == own_start + row, col >= total)
        offset = [near[k : k + 1, :] - mine[:, k : k + 1] for k in range(3)]
        square = offset[0] * offset[0] + offset[1] * offset[1] + offset[2] * offset[2]
        distance = jnp.sqrt(square + jnp.where(unused, 1.0, 0.0))
        inverse = 1.0 / distance
        smooth = 0.5 * (jnp.cos(math.pi / cutoff * distance) + 1.0)
        spots[0, :, rows] = distance
        spots[1, :, rows] = jnp.where(
            jnp.logical_and(distance < cutoff, jnp.logical_not(unused)), smooth, 0.0
        )
        for k in range(3):
            spots[k + 2, :, rows] = offset[k] * inverse
        half = jnp.dot(
            near_state[0, rows, :].astype(jnp.bfloat16),
            (0.5 * atom_in_all[layer].astype(jnp.float32)).astype(jnp.bfloat16),
            preferred_element_type=jnp.float32,
        ) + 0.5 * atom_bias_all[layer : layer + 1, :]
        hidden = (half + half * jnp.tanh(half)).astype(jnp.bfloat16)
        gates = jnp.dot(hidden, atom_out[...], preferred_element_type=jnp.float32).astype(
            jnp.bfloat16
        )
        plain_table[rows, :width] = gates[:, :width]
        gate_b = gates[:, width : 2 * width].astype(jnp.float32)
        gate_c = gates[:, 2 * width : 3 * width]
        gate_g = gates[:, 3 * width :].astype(jnp.float32)
        for part in range(3):
            vector = near_state[part + 1, rows, :]
            plain_table[rows, (part + 1) * width : (part + 2) * width] = (gate_b * vector).astype(
                jnp.bfloat16
            )
            turned_table[part, rows, :width] = gate_c
            turned_table[part, rows, width:] = (gate_g * vector).astype(jnp.bfloat16)

    own_count = counts[home, 0]
    fresh[...] = jnp.zeros(fresh.shape, fresh.dtype)
    sharpness = 0.5 * ((basis_count - 1) / cutoff) ** 2

    @pl.loop(0, lax.div(own_count + group - 1, group))
    def _(turn):
        first = pl.multiple_of(turn * group, group)

        def form_edges(step):
            columns = slice(step * chunk, (step + 1) * chunk)
            receivers = pl.ds(first, group)
            distance = spots[0, receivers, columns]
            centers = lax.broadcasted_iota(jnp.int32, (1, basis_count, chunk), 1).astype(
                jnp.float32
            ) * (cutoff / (basis_count - 1))
            gap = distance[:, None, :] - centers
            basis = jnp.exp(-sharpness * gap * gap).reshape(group * basis_count, chunk)
            half = jnp.dot(
                radial_blocks[layer],
                basis.astype(jnp.bfloat16),
                preferred_element_type=jnp.float32,
            ).reshape(group, hidden_width, chunk) + bias_wide[layer][None]
            active = (half + half * jnp.tanh(half)) * spots[1, receivers, columns][:, None, :]
            edges[0, :, columns] = active.reshape(group * hidden_width, chunk).astype(jnp.bfloat16)
            for k in range(3):
                unit = spots[k + 2, receivers, columns][:, None, :]
                edges[k + 1, :, columns] = (
                    (active * unit).reshape(group * hidden_width, chunk).astype(jnp.bfloat16)
                )

        for used in range(1, max_chunks + 1):

            @pl.when(chunks == used)
            def _(used=used):
                span = used * chunk
                for step in range(used):
                    form_edges(step)

                def contracted(left, right, filters):
                    product = jnp.dot(left, right, preferred_element_type=jnp.float32)
                    product = product.reshape(group, hidden_width, 2 * width)
                    return (
                        jnp.sum(product[:, :, :width] * filters[0], axis=1),
                        jnp.sum(product[:, :, width:] * filters[1], axis=1),
                    )

                bank = [
                    radial_out[:, part * width : (part + 1) * width].astype(jnp.float32)[None]
                    for part in range(4)
                ]
                flat = edges[0, :, :span]
                scalar, vector0 = contracted(flat, plain_table[:span, : 2 * width], (bank[0], bank[1]))
                vector1, vector2 = contracted(flat, plain_table[:span, 2 * width :], (bank[1], bank[1]))
                vectors = [vector0, vector1, vector2]
                for k in range(3):
                    along, project = contracted(
                        edges[k + 1, :, :span], turned_table[k, :span, :], (bank[2], bank[3])
                    )
                    vectors[k] = vectors[k] + along
                    scalar = scalar + project
                receivers = first + lax.broadcasted_iota(jnp.int32, (group, width), 0)
                alive = receivers < own_count
                for part, change in enumerate([scalar] + vectors):
                    before = near_state[part, pl.ds(own_start + first, group), :]
                    after = jnp.where(alive, before + message_scale * change, 0.0)
                    fresh[pl.ds(first, group), part * width : (part + 1) * width] = after

    rounded = fresh[...].astype(jnp.bfloat16)
    scalars_out[0, 0] = rounded[:, :width]
    for part in range(3):
        vectors_out[0, part] = rounded[:, (part + 1) * width : (part + 2) * width]
    if layer == radial_out_all.shape[0] - 1:
        read = lax.dot_general(
            rounded[:, :width],
            readout_in[...],
            (((1,), (1,)), ((), ())),
            preferred_element_type=jnp.float32,
        )
        read = read / (1.0 + jnp.exp(-read)) * readout_out[...]
        alive = lax.broadcasted_iota(jnp.int32, read.shape, 0) < own_count
        amount = jnp.sum(jnp.where(alive, read, 0.0), axis=(0, 1), keepdims=True)
        part_out[...] += jnp.broadcast_to(amount, part_out.shape)


def layer_update(layer, cells_shape, counts, places, states, params):
    cells_wide, cells_deep, cells_tall = cells_shape
    total_cells = cells_wide * cells_deep * cells_tall
    states = [state.reshape((-1,) + state.shape[3:]) for state in states]
    slots, width = states[0].shape[2:]
    hidden_width = params[1].shape[1]
    max_chunks = -(-27 * slots // chunk)
    span = max_chunks * chunk
    store = 27 * slots + chunk + slots
    store = -(-store // 8) * 8
    vmem = pl.BlockSpec(memory_space=pltpu.VMEM)
    return pl.pallas_call(
        functools.partial(layer_kernel, (cells_deep, cells_tall), max_chunks, layer),
        grid=(total_cells,),
        out_shape=(
            jax.ShapeDtypeStruct((total_cells, 1, slots, width), jnp.bfloat16),
            jax.ShapeDtypeStruct((total_cells, 3, slots, width), jnp.bfloat16),
            jax.ShapeDtypeStruct((8, 128), jnp.float32),
        ),
        in_specs=[pl.BlockSpec(memory_space=pltpu.SMEM)] + [vmem] * (3 + len(params)),
        out_specs=(
            pl.BlockSpec((1, 1, slots, width), lambda i: (i, 0, 0, 0)),
            pl.BlockSpec((1, 3, slots, width), lambda i: (i, 0, 0, 0)),
            pl.BlockSpec((8, 128), lambda i: (0, 0)),
        ),
        scratch_shapes=[
            pltpu.VMEM((slots, 4 * width), jnp.float32),
            pltpu.VMEM((5, slots, span), jnp.float32),
            pltpu.VMEM((store, width), jnp.float32),
            pltpu.VMEM((4, store, width), jnp.float32),
            pltpu.VMEM((4, group * hidden_width, span), jnp.bfloat16),
            pltpu.VMEM((span, 4 * width), jnp.bfloat16),
            pltpu.VMEM((3, span, 2 * width), jnp.bfloat16),
        ],
        compiler_params=pltpu.CompilerParams(vmem_limit_bytes=56 << 20),
        name="message_layer",
    )(counts, places, *states, *params)


def on_device(
    positions,
    counts,
    scalars,
    vectors,
    radial_in,
    radial_bias,
    radial_out,
    atom_in,
    atom_bias,
    atom_out,
    readout_in,
    readout_out,
):
    cells_wide, cells_deep, cells_tall, slots, width = scalars.shape
    cells_shape = (cells_wide, cells_deep, cells_tall)
    level = jnp.broadcast_to(counts.astype(jnp.float32)[..., None, None], cells_shape + (1, slots))
    geometry = jnp.concatenate([positions, level], axis=3)
    geometry = jnp.pad(geometry, ((0, 0),) * 3 + ((0, 8 - geometry.shape[3]), (0, 128 - slots)))
    geometry = geometry[:, :, :, None]
    states = [scalars[:, :, :, None], vectors.transpose(0, 1, 2, 4, 3, 5)]
    params = (radial_out, atom_in, atom_bias, atom_out, readout_in.T, readout_out[None, :])
    for layer in range(radial_in.shape[0]):
        if layer == 0:
            *states, places, near_counts, blocks, bias_wide = extended(
                states, 0, (geometry, radial_in, radial_bias)
            )
            params = (blocks, bias_wide) + params
        else:
            states = extended(states, layer)
        *states, part = layer_update(layer, cells_shape, near_counts, places, states, params)
        states = [state.reshape(cells_shape + state.shape[1:]) for state in states]
    scalar_state = states[0][:, :, :, 0]
    vector_state = states[1].transpose(0, 1, 2, 4, 3, 5)
    energy = summed(part, ("gz", "gx", "gy"), radial_in.shape[0])
    return (scalar_state, vector_state, energy)


def solution(mesh):
    block = P("gx", "gy", "gz")
    in_specs = (block,) * 4 + (P(),) * 8
    out_specs = (block, block, P())
    return jax.shard_map(
        on_device, mesh=mesh, in_specs=in_specs, out_specs=out_specs, check_vma=False
    )
```

profile of v0, /device:TPU:0, one launch (start us, length us, event | category | flops | bytes accessed | tf_op | source)
XLA Modules:
  0.0 83.4 jit_solution(2621066611972880871)
XLA Ops:
  0.6 0.0 copy-start.1
  0.6 0.0 copy-start
  0.6 0.6 copy-done.1
  1.3 0.1 broadcast_in_dim.19
  1.4 0.0 copy-done
  1.4 0.6 fusion.refs_2_
  2.0 21.7 %halo.2 = (bf16[4,3,3,1,32,128]{5,4,3,2,1,0:T(8,128)(2,1)}, bf16[4,3,3,3,32,128]{5,4,3,2,1,0:T(8,128)(2,1)}, f32[36,32,128]{2,1,0:T(8,128)}, s32[36,128]{1,0:T(8...) custom-call(bf16[2,1,1,1,32,128]{5,4,3,2,1,0:T(8,128)(2,1)} %bitcast.30, ...), custom_call_target="tpu_custom_call" | custom-call | tf_op jit(solution)/shard_map/halo/pallas_call | solution.py:147
  23.7 9.1 %message_layer.2 = (bf16[2,1,32,128]{3,2,1,0:T(8,128)(2,1)}, bf16[2,3,32,128]{3,2,1,0:T(8,128)(2,1)}, f32[8,128]{1,0:T(8,128)}) custom-call(s32[36,128]{1,0:T(8,128)} %get-tuple-element.16.counts, f32[36,32,128]{2,1,0:T(8,128)} %get-tuple-element.17.places, bf16[36,1,32,128]{3,2,1,0:T(8,128)(2,1)} %bitcast.25, bf16[36,3,32,128]{3,2,1,0:T(8,128)(2,1)} %bitcast.23, ...), custom_call_target="tpu_custom_call" | custom-call | tf_op jit(solution)/shard_map/message_layer/pallas_call | solution.py:429
  32.7 21.4 %halo.3 = (bf16[4,3,3,1,32,128]{5,4,3,2,1,0:T(8,128)(2,1)}, bf16[4,3,3,3,32,128]{5,4,3,2,1,0:T(8,128)(2,1)}) custom-call(bf16[2,1,1,1,32,128]{5,4,3,2,1,0:T(8,128)(2,1)} %bitcast.31, bf16[2,1,1,3,32,128]{5,4,3,2,1,0:T(8,128)(2,1)} %bitcast.29), custom_call_target="tpu_custom_call" | custom-call | tf_op jit(solution)/shard_map/halo/pallas_call | solution.py:147
  54.2 9.8 %message_layer.3 = (bf16[2,1,32,128]{3,2,1,0:T(8,128)(2,1)}, bf16[2,3,32,128]{3,2,1,0:T(8,128)(2,1)}, f32[8,128]{1,0:T(8,128)}) custom-call(s32[36,128]{1,0:T(8,128)} %get-tuple-element.16.counts, f32[36,32,128]{2,1,0:T(8,128)} %get-tuple-element.17.places, bf16[36,1,32,128]{3,2,1,0:T(8,128)(2,1)} %bitcast.24, bf16[36,3,32,128]{3,2,1,0:T(8,128)(2,1)} %bitcast.22, ...), custom_call_target="tpu_custom_call" | custom-call | tf_op jit(solution)/shard_map/message_layer/pallas_call | solution.py:429
  63.9 17.7 %total.1 = f32[1]{0:T(128)} custom-call(f32[8,128]{1,0:T(8,128)} %get-tuple-element.28.part), custom_call_target="tpu_custom_call" | custom-call | tf_op jit(solution)/shard_map/total/pallas_call | solution.py:205
  (2 shorter events, 0.0 us)
Async XLA Ops:
  0.6 0.7 copy-start.1
  0.6 0.7 copy-start
where the time goes:
time: 84.6 us; the launch traced here: 83.4 us
  Pallas kernels  79.7 us (94%)
  between operations  2.36 us (3%)
    pallas_call x2, Pallas kernels, extended(): pl.pallas_call(functools.partial(halo_kernel, bool(extra)), out_shape=sha...  43.1 us
    pallas_call x2, Pallas kernels, layer_update(): pl.pallas_call(functools.partial(layer_kernel, (cells_deep, cells_tall),...  18.9 us
    pallas_call x1, Pallas kernels, summed(): pl.pallas_call(functools.partial(total_kernel, axes), out_shape=jax.Shape...  17.7 us

commit v1 on v0

v1 whole, which is shorter than its diff:
```python
import functools
import itertools
import math

import jax
import jax.numpy as jnp
from jax import lax
from jax.experimental import pallas as pl
from jax.experimental.pallas import tpu as pltpu
from jax.sharding import PartitionSpec as P

cutoff = 5.0
message_scale = 0.5
group = 8
chunk = 256

MESH = pl.DeviceIdType.MESH


def beside(axis, step):
    count = lax.axis_size(axis)
    return lax.rem(lax.axis_index(axis) + step + count, count)


def prepare(near_ground, radial_in, radial_bias, tiles, places, counts, radial_block):
    tall, deep, wide = near_ground.shape[:3]
    cells = tall * deep * wide
    slots = places.shape[1]
    rows = near_ground[...].reshape(cells, 128)
    tiles[...] = jnp.zeros(tiles.shape, tiles.dtype)
    tiles[:cells, 0, :] = rows
    for part in range(1, 4):
        tiles[:cells, part, :] = jnp.concatenate(
            [rows[:, part * slots :], rows[:, : part * slots]], axis=1
        )
    lane = lax.broadcasted_iota(jnp.int32, (slots, 8), 1)
    for index, (z, y, x) in enumerate(itertools.product(range(tall), range(deep), range(wide))):
        shift = jnp.where(
            lane == 0, float(x - 1), jnp.where(lane == 1, float(y - 1), float(z - 1))
        )
        places[index, :, :8] = tiles[index].T[:slots, :] + shift * cutoff
    level = tiles[:, 3, :]
    counts[...] = level.T[:1, :].astype(jnp.int32)

    layers, basis_count, hidden_width = radial_in.shape
    box = (group, hidden_width, 128)
    owner = lax.div(lax.broadcasted_iota(jnp.int32, box, 2), basis_count)
    match = owner == lax.broadcasted_iota(jnp.int32, box, 0)
    column = lax.broadcasted_iota(jnp.int32, (hidden_width, 128), 1) - group * basis_count
    for layer in range(layers):
        small = 0.5 * radial_in[layer].astype(jnp.float32)
        tall_form = jnp.concatenate([small] * (128 // basis_count), axis=0)
        wide_form = jnp.concatenate([tall_form] * (128 // hidden_width), axis=1).T[:hidden_width]
        bias = 0.5 * radial_bias[layer : layer + 1, :]
        bias = jnp.concatenate([bias] * (128 // hidden_width), axis=1)
        bias = jnp.broadcast_to(bias, (128, 128)).T[:hidden_width]
        high = bias.astype(jnp.bfloat16).astype(jnp.float32)
        middle = (bias - high).astype(jnp.bfloat16).astype(jnp.float32)
        low = bias - high - middle
        offset = jnp.where(
            column == 0, high, jnp.where(column == 1, middle, jnp.where(column == 2, low, 0.0))
        )
        spread = jnp.where(match, jnp.broadcast_to(wide_form[None], box), 0.0) + offset[None]
        radial_block[layer] = spread.reshape(radial_block.shape[1:]).astype(jnp.bfloat16)


def halo_kernel(first, dims, *refs):
    wide, deep, tall = dims
    if first:
        scalars, vectors, ground, radial_in, radial_bias = refs[:5]
        near, places, counts, radial_block = refs[5:9]
        near_ground, tiles, own_sem, send_sem, recv_sem = refs[9:]
    else:
        block, near, own_sem, send_sem, recv_sem = refs
    sides = [side for side in itertools.product((0, -1, 1), (0, -1, 1)) if side != (0, 0)]
    barrier = pltpu.get_barrier_semaphore()
    for dx, dy in sides:
        pl.semaphore_signal(
            barrier,
            inc=1,
            device_id={"gx": beside("gx", dx), "gy": beside("gy", dy)},
            device_id_type=MESH,
        )
    for dz in (-1, 1):
        pl.semaphore_signal(
            barrier, inc=1, device_id={"gz": beside("gz", dz)}, device_id_type=MESH
        )

    inner = tuple(pl.ds(1, extent) for extent in (tall, deep, wide))
    own = []
    if first:
        own.append(pltpu.make_async_copy(scalars, near.at[inner + (pl.ds(0, 1),)], own_sem.at[0]))
        own.append(pltpu.make_async_copy(vectors, near.at[inner + (pl.ds(1, 3),)], own_sem.at[1]))
        own.append(pltpu.make_async_copy(ground, near_ground.at[inner], own_sem.at[2]))
    else:
        own.append(pltpu.make_async_copy(block, near.at[inner], own_sem.at[0]))
    for copy in own:
        copy.start()
    pl.semaphore_wait(barrier, len(sides) + 2)

    def span(extent, side):
        if side == 0:
            return pl.ds(1, extent), pl.ds(1, extent)
        if side > 0:
            return pl.ds(extent, 1), pl.ds(0, 1)
        return pl.ds(1, 1), pl.ds(extent + 1, 1)

    copies = []

    def send(source, target, device):
        number = len(copies)
        copy = pltpu.make_async_remote_copy(
            src_ref=source,
            dst_ref=target,
            send_sem=send_sem.at[number],
            recv_sem=recv_sem.at[number],
            device_id=device,
            device_id_type=MESH,
        )
        copy.start()
        copies.append(copy)
        return copy

    def inward(at):
        return pl.ds(at.start - 1, at.size)

    def along_plane(dx, dy):
        from_x, to_x = span(wide, dx)
        from_y, to_y = span(deep, dy)
        device = {"gx": beside("gx", dx), "gy": beside("gy", dy)}
        every = pl.ds(1, tall)
        begin = (pl.ds(0, tall), inward(from_y), inward(from_x))
        sent = []
        if first:
            sent.append(send(ground.at[begin], near_ground.at[every, to_y, to_x], device))
            sent.append(
                send(scalars.at[begin], near.at[every, to_y, to_x, pl.ds(0, 1)], device)
            )
            sent.append(
                send(vectors.at[begin], near.at[every, to_y, to_x, pl.ds(1, 3)], device)
            )
        else:
            sent.append(send(block.at[begin], near.at[every, to_y, to_x], device))
        return sent

    def across(dx, dy, whole):
        at_x, at_y = span(wide, dx)[1], span(deep, dy)[1]
        pieces = [near]
        if first:
            pieces = [near_ground, near]
        sent = []
        for dz in (-1, 1):
            from_z, to_z = span(tall, dz)
            device = {"gz": beside("gz", dz)}
            if whole:
                begin = (inward(from_z), pl.ds(0, deep), pl.ds(0, wide))
                if first:
                    sent.append(send(ground.at[begin], near_ground.at[to_z, at_y, at_x], device))
                    sent.append(
                        send(scalars.at[begin], near.at[to_z, at_y, at_x, pl.ds(0, 1)], device)
                    )
                    sent.append(
                        send(vectors.at[begin], near.at[to_z, at_y, at_x, pl.ds(1, 3)], device)
                    )
                else:
                    sent.append(send(block.at[begin], near.at[to_z, at_y, at_x], device))
            else:
                for ref in pieces:
                    sent.append(
                        send(ref.at[from_z, at_y, at_x], ref.at[to_z, at_y, at_x], device)
                    )
        return sent

    order = [(0, -1), (0, 1), (1, 0), (-1, 0), (1, -1), (-1, -1), (1, 1), (-1, 1)]
    direct = {side: along_plane(*side) for side in order[:2]}
    last = [across(0, 0, True)]
    for side in order[2:]:
        direct[side] = along_plane(*side)
    for side in order:
        for copy in direct[side]:
            copy.wait_recv()
        last.append(across(*side, False))
    if first:
        own.pop().wait()
        for sent in last:
            share = len(sent) // 2
            sent[share].wait_recv()
            sent[0].wait_recv()
        prepare(near_ground, radial_in, radial_bias, tiles, places, counts, radial_block)
    for sent in last:
        share = len(sent) // 2
        for place, copy in enumerate(sent):
            if not first or place % share:
                copy.wait_recv()
    for copy in own:
        copy.wait()
    for copy in copies:
        copy.wait_send()


def extended(states, dims, identity, extra=()):
    wide, deep, tall = dims
    slots, width = states[0].shape[-2:]
    vmem = pl.BlockSpec(memory_space=pltpu.VMEM)
    anywhere = pl.BlockSpec(memory_space=pl.ANY)
    outer = (tall + 2, deep + 2, wide + 2)
    cells = math.prod(outer)
    shapes = [jax.ShapeDtypeStruct(outer + (4, slots, width), states[0].dtype)]
    out_specs = [anywhere]
    in_specs = [anywhere] * len(states)
    scratch = []
    pieces = 26
    if extra:
        layers, basis_count, hidden_width = extra[1].shape
        shapes += [
            jax.ShapeDtypeStruct((cells, slots, 128), jnp.float32),
            jax.ShapeDtypeStruct((1, 128), jnp.int32),
            jax.ShapeDtypeStruct((layers, group * hidden_width, 128), jnp.bfloat16),
        ]
        out_specs += [vmem] * 3
        in_specs += [vmem] * 3
        scratch = [
            pltpu.VMEM(outer + (1, 128), jnp.float32),
            pltpu.VMEM((128, 8, 128), jnp.float32),
        ]
        pieces = 8 * 3 + 2 * 3 + 16 * 2
    return pl.pallas_call(
        functools.partial(halo_kernel, bool(extra), dims),
        out_shape=shapes,
        in_specs=in_specs,
        out_specs=out_specs,
        scratch_shapes=scratch
        + [
            pltpu.SemaphoreType.DMA((3,)),
            pltpu.SemaphoreType.DMA((pieces,)),
            pltpu.SemaphoreType.DMA((pieces,)),
        ],
        compiler_params=pltpu.CompilerParams(
            collective_id=identity, has_side_effects=True, vmem_limit_bytes=56 << 20
        ),
        name="halo",
    )(*states, *extra)


def total_kernel(axes, part, out, held, local_sem, send_sem, recv_sem):
    sizes = [lax.axis_size(axis) for axis in axes]
    places = [lax.axis_index(axis) for axis in axes]
    count = math.prod(sizes)
    barrier = pltpu.get_barrier_semaphore()

    def partner(step):
        device = {}
        for axis, size, me in zip(axes, sizes, places):
            device[axis] = lax.rem(me + lax.rem(step, size), size)
            step = lax.div(step, size)
        return device

    def greet(step, carry):
        pl.semaphore_signal(barrier, inc=1, device_id=partner(step), device_id_type=MESH)
        return carry

    lax.fori_loop(1, count, greet, 0)
    own = pltpu.make_async_copy(part, held.at[pl.ds(0, 1)], local_sem)
    own.start()
    pl.semaphore_wait(barrier, count - 1)

    def copy(step):
        return pltpu.make_async_remote_copy(
            src_ref=part,
            dst_ref=held.at[pl.ds(step, 1)],
            send_sem=send_sem.at[step],
            recv_sem=recv_sem.at[step],
            device_id=partner(step),
            device_id_type=MESH,
        )

    def send(step, carry):
        copy(step).start()
        return carry

    def settle(step, carry):
        copy(step).wait()
        return carry

    lax.fori_loop(1, count, send, 0)
    own.wait()
    lax.fori_loop(1, count, settle, 0)
    out[0] = jnp.sum(held[...])


def summed(part, axes, identity):
    count = math.prod(lax.axis_size(axis) for axis in axes)
    vmem = pl.BlockSpec(memory_space=pltpu.VMEM)
    return pl.pallas_call(
        functools.partial(total_kernel, axes),
        out_shape=jax.ShapeDtypeStruct((1,), part.dtype),
        in_specs=[vmem],
        out_specs=pl.BlockSpec(memory_space=pltpu.SMEM),
        scratch_shapes=[
            pltpu.VMEM((count,) + part.shape[1:], part.dtype),
            pltpu.SemaphoreType.DMA,
            pltpu.SemaphoreType.DMA((count,)),
            pltpu.SemaphoreType.DMA((count,)),
        ],
        compiler_params=pltpu.CompilerParams(
            collective_id=identity, has_side_effects=True, vmem_limit_bytes=56 << 20
        ),
        name="total",
    )(part)


def layer_kernel(dims, max_chunks, basis_count, layer, last, *refs):
    counts, places, near, radial_blocks, radial_out_all, atom_in_all = refs[:6]
    atom_bias_all, atom_out_all, readout_in, readout_out = refs[6:10]
    if last:
        scalars_out, vectors_out, part_out = refs[10:13]
    else:
        (block_out,) = refs[10:11]
    fresh, near_place, spots, near_state, edges_even, edges_odd, plain_table, turned_table = refs[-8:]
    wide, deep, tall = dims
    slots, width = near.shape[2:]
    radial_out = radial_out_all.at[layer]
    atom_out = atom_out_all.at[layer]
    hidden_width = radial_out.shape[0]

    inside = [
        (z, y, x)
        for z in range(1, tall + 1)
        for y in range(1, deep + 1)
        for x in range(1, wide + 1)
    ]
    outside = [
        place
        for place in itertools.product(range(tall + 2), range(deep + 2), range(wide + 2))
        if place not in inside
    ]
    total = 0
    starts = []
    for place in inside + outside:
        index = (place[0] * (deep + 2) + place[1]) * (wide + 2) + place[2]
        rows = pl.ds(total, slots)
        near_place[rows, :] = places[index]
        for part in range(4):
            near_state[part, rows, :] = near[index, part].astype(jnp.float32)
        starts.append(total)
        total = total + counts[0, index]
    own_total = starts[len(inside)]
    blank = jnp.zeros((chunk, width), jnp.float32)
    near_place[pl.ds(total, chunk), :] = blank
    for part in range(4):
        near_state[part, pl.ds(total, chunk), :] = blank
    chunks = lax.div(total + chunk - 1, chunk)

    receivers = wide * deep * tall * slots
    quarter = math.pi / cutoff

    @pl.loop(0, chunks)
    def _(step):
        rows = pl.ds(pl.multiple_of(step * chunk, chunk), chunk)
        line = near_place[rows, :].T[:8, :]
        mine = near_place[:receivers, :]
        col = step * chunk + lax.broadcasted_iota(jnp.int32, (receivers, chunk), 1)
        row = lax.broadcasted_iota(jnp.int32, (receivers, chunk), 0)
        unused = jnp.logical_or(col == row, col >= total)
        offset = [line[k : k + 1, :] - mine[:, k : k + 1] for k in range(3)]
        square = offset[0] * offset[0] + offset[1] * offset[1] + offset[2] * offset[2]
        distance = jnp.sqrt(square + jnp.where(unused, 1.0, 0.0))
        inverse = 1.0 / distance
        angle = quarter * distance - 0.5 * math.pi
        turn = angle * angle
        series = 0.0
        for power in (13, 11, 9, 7, 5, 3):
            series = turn * (series + (-1.0) ** (power // 2) / math.factorial(power))
        smooth = 0.5 - 0.5 * (angle + angle * series)
        spots[0, :receivers, rows] = distance
        spots[1, :receivers, rows] = jnp.where(
            jnp.logical_and(distance < cutoff, jnp.logical_not(unused)), smooth, 0.0
        )
        for k in range(3):
            spots[k + 2, :receivers, rows] = offset[k] * inverse
        half = jnp.dot(
            near_state[0, rows, :].astype(jnp.bfloat16),
            (0.5 * atom_in_all[layer].astype(jnp.float32)).astype(jnp.bfloat16),
            preferred_element_type=jnp.float32,
        ) + 0.5 * atom_bias_all[layer : layer + 1, :]
        hidden = (half + half * jnp.tanh(half)).astype(jnp.bfloat16)
        gates = jnp.dot(hidden, atom_out[...], preferred_element_type=jnp.float32).astype(
            jnp.bfloat16
        )
        plain_table[rows, :width] = gates[:, :width]
        gate_b = gates[:, width : 2 * width].astype(jnp.float32)
        gate_c = gates[:, 2 * width : 3 * width]
        gate_g = gates[:, 3 * width :].astype(jnp.float32)
        for part in range(3):
            vector = near_state[part + 1, rows, :]
            plain_table[rows, (part + 1) * width : (part + 2) * width] = (gate_b * vector).astype(
                jnp.bfloat16
            )
            turned_table[part, rows, :width] = gate_c
            turned_table[part, rows, width:] = (gate_g * vector).astype(jnp.bfloat16)

    sharpness = 0.5 * ((basis_count - 1) / cutoff) ** 2
    tile = 16

    def form_edges(first, columns, edges):
        these = pl.ds(first, group)
        centers = lax.broadcasted_iota(jnp.int32, (1, basis_count, chunk), 1).astype(
            jnp.float32
        ) * (cutoff / (basis_count - 1))
        gap = spots[0, these, columns][:, None, :] - centers
        basis = jnp.exp(-sharpness * gap * gap).reshape(group * basis_count, chunk)
        basis = jnp.concatenate(
            [basis, jnp.ones((128 - group * basis_count, chunk), jnp.float32)], axis=0
        )
        half = jnp.dot(
            radial_blocks[layer],
            basis.astype(jnp.bfloat16),
            preferred_element_type=jnp.float32,
        ).reshape(group, hidden_width, chunk)
        active = (half + half * jnp.tanh(half)) * spots[1, these, columns][:, None, :]
        active = active.astype(jnp.bfloat16).reshape(group, hidden_width // tile, tile, chunk)
        edges[0] = active.reshape(group * hidden_width, chunk)
        for k in range(3):
            unit = jnp.broadcast_to(
                spots[k + 2, these, columns][:, None, :], (group, tile, chunk)
            ).astype(jnp.bfloat16)
            edges[k + 1] = (active * unit[:, None]).reshape(group * hidden_width, chunk)

    def contract(first, rows, edges):
        def contracted(left, right, filters):
            product = jnp.dot(left, right, preferred_element_type=jnp.float32)
            product = product.reshape(group, hidden_width, 2 * width)
            return (
                jnp.sum(product[:, :, :width] * filters[0], axis=1),
                jnp.sum(product[:, :, width:] * filters[1], axis=1),
            )

        bank = [
            radial_out[:, part * width : (part + 1) * width].astype(jnp.float32)[None]
            for part in range(4)
        ]
        flat = edges[0]
        scalar, vector0 = contracted(flat, plain_table[rows, : 2 * width], (bank[0], bank[1]))
        vector1, vector2 = contracted(flat, plain_table[rows, 2 * width :], (bank[1], bank[1]))
        vectors = [vector0, vector1, vector2]
        for k in range(3):
            along, project = contracted(
                edges[k + 1], turned_table[k, rows, :], (bank[2], bank[3])
            )
            vectors[k] = vectors[k] + along
            scalar = scalar + project
        for part, change in enumerate([scalar] + vectors):
            fresh[part, pl.ds(first, group), :] += change

    groups = lax.div(own_total + group - 1, group)
    fresh[...] = jnp.zeros(fresh.shape, fresh.dtype)

    def place_of(task):
        turn = lax.div(task, chunks)
        step = task - turn * chunks
        first = pl.multiple_of(turn * group, group)
        return first, pl.ds(pl.multiple_of(step * chunk, chunk), chunk)

    tasks = groups * chunks

    @pl.loop(0, tasks)
    def _(task):
        first, rows = place_of(task)
        form_edges(first, rows, edges_even)
        contract(first, rows, edges_even)
    energy = jnp.zeros((1, 1), jnp.float32)
    for number, (place, start) in enumerate(zip(inside, starts)):
        index = (place[0] * (deep + 2) + place[1]) * (wide + 2) + place[2]
        alive = lax.broadcasted_iota(jnp.int32, (slots, width), 0) < counts[0, index]
        rounded = [
            jnp.where(
                alive,
                near_state[part, pl.ds(start, slots), :]
                + message_scale * fresh[part, pl.ds(start, slots), :],
                0.0,
            ).astype(jnp.bfloat16)
            for part in range(4)
        ]
        if last:
            scalars_out[number] = rounded[0]
            for part in range(3):
                vectors_out[number, part] = rounded[part + 1]
            read = lax.dot_general(
                rounded[0],
                readout_in[...],
                (((1,), (1,)), ((), ())),
                preferred_element_type=jnp.float32,
            )
            read = read / (1.0 + jnp.exp(-read)) * readout_out[...]
            read = jnp.where(alive[:, : read.shape[1]], read, 0.0)
            energy = energy + jnp.sum(read, axis=(0, 1), keepdims=True)
        else:
            for part in range(4):
                block_out[number, part] = rounded[part]
    if last:
        spot = lax.broadcasted_iota(jnp.int32, part_out.shape, 1)
        part_out[...] = jnp.where(spot == 0, jnp.broadcast_to(energy, part_out.shape), 0.0)


def layer_update(layer, dims, basis_count, counts, places, near, params):
    wide, deep, tall = dims
    near = near.reshape((-1,) + near.shape[3:])
    around = near.shape[0]
    slots, width = near.shape[2:]
    hidden_width = params[1].shape[1]
    last = layer == params[1].shape[0] - 1
    cells = wide * deep * tall
    max_chunks = -(-around * slots // chunk)
    span = max_chunks * chunk
    store = around * slots + chunk + slots
    receivers = cells * slots
    vmem = pl.BlockSpec(memory_space=pltpu.VMEM)
    if last:
        shapes = (
            jax.ShapeDtypeStruct((cells, slots, width), jnp.bfloat16),
            jax.ShapeDtypeStruct((cells, 3, slots, width), jnp.bfloat16),
            jax.ShapeDtypeStruct((1, 128), jnp.float32),
        )
    else:
        shapes = (jax.ShapeDtypeStruct((cells, 4, slots, width), jnp.bfloat16),)
    return pl.pallas_call(
        functools.partial(layer_kernel, dims, max_chunks, basis_count, layer, last),
        out_shape=shapes,
        in_specs=[pl.BlockSpec(memory_space=pltpu.SMEM)] + [vmem] * (2 + len(params)),
        out_specs=tuple(vmem for _ in shapes),
        scratch_shapes=[
            pltpu.VMEM((4, receivers + slots, width), jnp.float32),
            pltpu.VMEM((store, width), jnp.float32),
            pltpu.VMEM((5, receivers + 2 * group, span), jnp.float32),
            pltpu.VMEM((4, store, width), jnp.float32),
            pltpu.VMEM((4, group * hidden_width, chunk), jnp.bfloat16),
            pltpu.VMEM((4, group * hidden_width, chunk), jnp.bfloat16),
            pltpu.VMEM((span, 4 * width), jnp.bfloat16),
            pltpu.VMEM((3, span, 2 * width), jnp.bfloat16),
        ],
        compiler_params=pltpu.CompilerParams(vmem_limit_bytes=56 << 20),
        name="message_layer",
    )(counts, places, near, *params)


def on_device(
    positions,
    counts,
    scalars,
    vectors,
    radial_in,
    radial_bias,
    radial_out,
    atom_in,
    atom_bias,
    atom_out,
    readout_in,
    readout_out,
):
    dims = scalars.shape[:3]
    slots, width = scalars.shape[3:]
    level = counts.astype(jnp.float32)[..., None]
    ground = jnp.concatenate([positions.reshape(dims + (3 * slots,)), level], axis=3)
    ground = jnp.pad(ground, ((0, 0),) * 3 + ((0, 128 - ground.shape[3]),))
    ground = ground.transpose(2, 1, 0, 3)[:, :, :, None]
    states = [
        scalars.transpose(2, 1, 0, 3, 4)[:, :, :, None],
        vectors.transpose(2, 1, 0, 4, 3, 5),
    ]
    params = (radial_out, atom_in, atom_bias, atom_out, readout_in.T, readout_out[None, :])
    near, places, near_counts, blocks = extended(states, dims, 0, (ground, radial_in, radial_bias))
    params = (blocks,) + params
    layers = radial_in.shape[0]
    turned = dims[::-1]
    for layer in range(layers):
        made = layer_update(layer, dims, radial_in.shape[1], near_counts, places, near, params)
        if layer < layers - 1:
            (near,) = extended([made[0].reshape(turned + (4, slots, width))], dims, layer + 1)
    new_scalars, new_vectors, part = made
    scalar_state = new_scalars.reshape(turned + (slots, width)).transpose(2, 1, 0, 3, 4)
    vector_state = new_vectors.reshape(turned + (3, slots, width)).transpose(2, 1, 0, 4, 3, 5)
    energy = summed(part, ("gx", "gy", "gz"), layers)
    return (scalar_state, vector_state, energy)


def solution(mesh):
    block = P("gx", "gy", "gz")
    in_specs = (block,) * 4 + (P(),) * 8
    out_specs = (block, block, P())
    return jax.shard_map(
        on_device, mesh=mesh, in_specs=in_specs, out_specs=out_specs, check_vma=False
    )
```

time: 84.6 us -> 74.5 us (0.88)
  Pallas kernels: 79.7 us -> 68.4 us
  other arithmetic: 0.61 us -> 2 us
    pallas_call x4, Pallas kernels: 61.9 us -> 55 us  [the longest x2 42.6 us: extended(): pl.pallas_call(functools.partial(halo_kernel, bool(extra), dims), out_sha...]
    pallas_call x1, Pallas kernels: 17.7 us -> 13.5 us  [summed(): pl.pallas_call(functools.partial(total_kernel, axes), out_shape=jax.Shape...]
where the time goes in v1:
time: 74.5 us; the launch traced here: 73.1 us
  Pallas kernels  68.4 us (92%)
  between operations  2.47 us (3%)
  other arithmetic  2 us (3%)
    pallas_call x2, Pallas kernels, extended(): pl.pallas_call(functools.partial(halo_kernel, bool(extra), dims), out_sha...  42.6 us
    pallas_call x1, Pallas kernels, summed(): pl.pallas_call(functools.partial(total_kernel, axes), out_shape=jax.Shape...  13.5 us
    pallas_call x2, Pallas kernels, layer_update(): pl.pallas_call(functools.partial(layer_kernel, dims, max_chunks, basis_co...  12.3 us

profile of v1, /device:TPU:0, one launch (start us, length us, event | category | flops | bytes accessed | tf_op | source)
XLA Modules:
  0.0 73.1 jit_solution(6639935193620745065)
XLA Ops:
  0.6 0.7 convert_bitcast_fusion
  1.3 0.1 copy.16
  1.4 0.7 reduce
  2.1 0.1 reshape.21
  2.2 0.6 select_maximum_fusion
  2.8 19.4 %halo.2 = (bf16[3,3,4,4,32,128]{5,4,3,2,1,0:T(8,128)(2,1)}, f32[36,32,128]{2,1,0:T(8,128)}, s32[1,128]{1,0:T(1,128)}, bf16[2,512,128]{2,1,0:T(8,128)(2,1)}) custom-call(bf16[1,1,2,1,32,128]{5,4,3,2,1,0:T(8,128)(2,1)} %bitcast.26, bf16[1,1,2,3,32,128]{5,4,3,2,1,0:T(8,128)(2,1)} %bitcast.25, f32[1,1,2,1,128]{4,3,2,1,0:T(1,128)} %bitcast.27, ...), custom_call_target="tpu_custom_call" | custom-call | tf_op jit(solution)/shard_map/halo/pallas_call | solution.py:227
  22.2 6.1 %message_layer.2 = bf16[2,4,32,128]{3,2,1,0:T(8,128)(2,1)} custom-call(s32[1,128]{1,0:T(1,128)} %get-tuple-element.10.refs_0_, f32[36,32,128]{2,1,0:T(8,128)} %get-tuple-element.11.refs_1_, bf16[36,4,32,128]{3,2,1,0:T(8,128)(2,1)} %bitcast.21, bf16[2,512,128]{2,1,0:T(8,128)(2,1)} %get-tuple-element.13.refs_3_, bf16[2,64,512]{2,1,0:T(8,128)(2,1)} %refs_4_.5, ...), custom_call_target="tpu_custom_call" | custom-call | tf_op jit(solution)/shard_map/message_layer/pallas_call | solution.py:526
  28.3 23.2 %halo.3 = bf16[3,3,4,4,32,128]{5,4,3,2,1,0:T(8,128)(2,1)} custom-call(bf16[1,1,2,4,32,128]{5,4,3,2,1,0:T(8,128)(2,1)} %bitcast.22), custom_call_target="tpu_custom_call" | custom-call | tf_op jit(solution)/shard_map/halo/pallas_call | solution.py:227
  51.6 6.2 %message_layer.3 = (bf16[2,32,128]{2,1,0:T(8,128)(2,1)}, bf16[2,3,32,128]{3,2,1,0:T(8,128)(2,1)}, f32[1,128]{1,0:T(1,128)}) custom-call(s32[1,128]{1,0:T(1,128)} %get-tuple-element.10.refs_0_, f32[36,32,128]{2,1,0:T(8,128)} %get-tuple-element.11.refs_1_, bf16[36,4,32,128]{3,2,1,0:T(8,128)(2,1)} %bitcast.20, bf16[2,512,128]{2,1,0:T(8,128)(2,1)} %get-tuple-element.13.refs_3_, ...), custom_call_target="tpu_custom_call" | custom-call | tf_op jit(solution)/shard_map/message_layer/pallas_call | solution.py:526
  57.8 13.5 %total.1 = f32[1]{0:T(128)} custom-call(f32[1,128]{1,0:T(1,128)} %get-tuple-element.16.part), custom_call_target="tpu_custom_call" | custom-call | tf_op jit(solution)/shard_map/total/pallas_call | solution.py:294

commit v2 on v1

v2 whole, which is shorter than its diff:
```python
import functools
import itertools
import math

import jax
import jax.numpy as jnp
from jax import lax
from jax.experimental import pallas as pl
from jax.experimental.pallas import tpu as pltpu
from jax.sharding import PartitionSpec as P

cutoff = 5.0
message_scale = 0.5
group = 8
chunk = 512
table_chunk = 256
shares = 4

MESH = pl.DeviceIdType.MESH


def beside(axis, step):
    count = lax.axis_size(axis)
    return lax.rem(lax.axis_index(axis) + step + count, count)


def prepare(near_ground, radial_in, radial_bias, tiles, places, counts, radial_block):
    tall, deep, wide = near_ground.shape[:3]
    cells = tall * deep * wide
    slots = places.shape[1]
    rows = near_ground[...].reshape(cells, 128)
    tiles[...] = jnp.zeros(tiles.shape, tiles.dtype)
    tiles[:cells, 0, :] = rows
    for part in range(1, 4):
        tiles[:cells, part, :] = jnp.concatenate(
            [rows[:, part * slots :], rows[:, : part * slots]], axis=1
        )
    lane = lax.broadcasted_iota(jnp.int32, (slots, 8), 1)
    for index, (z, y, x) in enumerate(itertools.product(range(tall), range(deep), range(wide))):
        shift = jnp.where(
            lane == 0, float(x - 1), jnp.where(lane == 1, float(y - 1), float(z - 1))
        )
        places[index, :, :8] = tiles[index].T[:slots, :] + shift * cutoff
    level = tiles[:, 3, :]
    counts[...] = level.T[:1, :].astype(jnp.int32)

    layers, basis_count, hidden_width = radial_in.shape
    box = (group, hidden_width, 128)
    owner = lax.div(lax.broadcasted_iota(jnp.int32, box, 2), basis_count)
    match = owner == lax.broadcasted_iota(jnp.int32, box, 0)
    column = lax.broadcasted_iota(jnp.int32, (hidden_width, 128), 1) - group * basis_count
    for layer in range(layers):
        small = 0.5 * radial_in[layer].astype(jnp.float32)
        tall_form = jnp.concatenate([small] * (128 // basis_count), axis=0)
        wide_form = jnp.concatenate([tall_form] * (128 // hidden_width), axis=1).T[:hidden_width]
        bias = 0.5 * radial_bias[layer : layer + 1, :]
        bias = jnp.concatenate([bias] * (128 // hidden_width), axis=1)
        bias = jnp.broadcast_to(bias, (128, 128)).T[:hidden_width]
        high = bias.astype(jnp.bfloat16).astype(jnp.float32)
        middle = (bias - high).astype(jnp.bfloat16).astype(jnp.float32)
        low = bias - high - middle
        offset = jnp.where(
            column == 0, high, jnp.where(column == 1, middle, jnp.where(column == 2, low, 0.0))
        )
        spread = jnp.where(match, jnp.broadcast_to(wide_form[None], box), 0.0) + offset[None]
        radial_block[layer] = spread.reshape(radial_block.shape[1:]).astype(jnp.bfloat16)


def halo_kernel(first, dims, *refs):
    wide, deep, tall = dims
    if first:
        level, positions, scalars, vectors, radial_in, radial_bias = refs[:6]
        near, places, counts, radial_block = refs[6:10]
        near_ground, tiles, own_sem, send_sem, recv_sem = refs[10:]
        held = ((scalars, pl.ds(0, 1)), (vectors, pl.ds(1, 3)))
    else:
        block, near, own_sem, send_sem, recv_sem = refs
        held = ((block, pl.ds(0, 4)),)
    barrier = pltpu.get_barrier_semaphore()
    for axis in ("gy", "gx", "gz"):
        for step in (-1, 1):
            pl.semaphore_signal(
                barrier, inc=1, device_id={axis: beside(axis, step)}, device_id_type=MESH
            )
    extents = {"gz": tall, "gy": deep, "gx": wide}
    axes = ("gz", "gy", "gx")
    inner = tuple(pl.ds(1, extents[axis]) for axis in axes)
    own = []
    for place, (state, part) in enumerate(held):
        own.append(
            pltpu.make_async_copy(state, near.at[inner + (part,)], own_sem.at[place])
        )
        own[-1].start()
    if first:
        slots = positions.shape[-1]
        for z, y, x in itertools.product(range(tall), range(deep), range(wide)):
            at = (x * deep + y) * tall + z
            row = [positions[at * 3 + k] for k in range(3)]
            row.append(jnp.full((1, 128 - 3 * slots), level[at], jnp.int32).astype(jnp.float32))
            near_ground[z + 1, y + 1, x + 1] = jnp.concatenate(row, axis=1)
    pl.semaphore_wait(barrier, 6)

    copies = []

    def send(ref, start, axis, step, region):
        extent = extents[axis]
        source, target = (extent, 0) if step > 0 else (1, extent + 1)
        return post(ref, start, axis, step, source, target, region)

    def post(ref, start, axis, step, source, target, region):
        begin, end = dict(region), dict(region)
        begin[axis], end[axis] = pl.ds(source, 1), pl.ds(target, 1)
        begin = [begin[name] for name in axes]
        if start is not None:
            begin = [pl.ds(at.start - 1, at.size) for at in begin]
        number = len(copies)
        copy = pltpu.make_async_remote_copy(
            src_ref=(ref if start is None else start).at[tuple(begin)],
            dst_ref=ref.at[tuple(end[name] for name in axes)],
            send_sem=send_sem.at[number],
            recv_sem=recv_sem.at[number],
            device_id={axis: beside(axis, step)},
            device_id_type=MESH,
        )
        copy.start()
        copies.append(copy)
        return copy

    def both(ref, start, axis, region):
        return [send(ref, start, axis, step, region) for step in (-1, 1)]

    def arrive(sent):
        for copy in sent:
            copy.wait_recv()

    odd = lax.rem(lax.axis_index("gz"), 2)
    own_part = {axis: pl.ds(1, extents[axis]) for axis in axes}
    every = {axis: pl.ds(0, extents[axis] + 2) for axis in axes}
    edge = {axis: {-1: pl.ds(extents[axis] + 1, 1), 1: pl.ds(0, 1)} for axis in axes}
    last = []

    mate = 1 - 2 * odd

    def aside(ref, start, step, region):
        flip = odd if step > 0 else 1 - odd
        source, target = tall + flip * (1 - tall), flip * (tall + 1)
        return post(ref, start, "gz", step * mate, source, target, region)

    def begin(axis, step, out, region):
        if not first:
            return [out(near, block, axis, step, region)]
        return [
            out(near.at[:, :, :, part], state, axis, step, region)
            for state, part in ((vectors, pl.ds(1, 3)), (scalars, pl.ds(0, 1)))
        ]

    def sideways(ref, start, axis, step, region):
        return aside(ref, start, step, region)

    def outward(x, region):
        steps = [step for step, place in ((-1, 1), (1, wide)) if place == x]
        return [(step, send(near, None, "gx", step, region)) for step in steps]

    sides = [(x, step) for x in range(1, wide + 1) for step in (-1, 1)]
    along_y, along_x = {}, {}
    if first:
        ground_y = both(near_ground, None, "gy", own_part)
    for x, step in sides:
        along_y[x, step] = begin("gy", step, send, {**own_part, "gx": pl.ds(x, 1)})
    for step in (-1, 1):
        last += begin("gz", step, sideways, own_part)
    for step in (-1, 1):
        along_x[step] = begin("gx", step, send, own_part)
    if first:
        arrive(ground_y)
        ground_x = both(near_ground, None, "gx", {**own_part, "gy": every["gy"]})
    for step in (-1, 1):
        arrive(along_x[step])
        region = {**own_part, "gx": edge["gx"][step]}
        last += [aside(near, None, -1, region), aside(near, None, 1, region)]
    crossed, turned = {}, []
    for x, step in sides:
        arrive(along_y[x, step])
        region = {**own_part, "gy": edge["gy"][step], "gx": pl.ds(x, 1)}
        crossed[x, step] = aside(near, None, -1, region)
        turned += [(step, *sent) for sent in outward(x, region)]
        last.append(aside(near, None, 1, region))
    if first:
        arrive(ground_x)
        last_ground = both(near_ground, None, "gz", {**every})
    far = pl.ds(odd * (tall + 1), 1)
    for (x, step), copy in crossed.items():
        arrive([copy])
        region = {"gy": edge["gy"][step], "gx": pl.ds(x, 1), "gz": far}
        last += [copy for _, copy in outward(x, region)]
    for step, step_x, copy in turned:
        arrive([copy])
        region = {**own_part, "gy": edge["gy"][step], "gx": edge["gx"][step_x]}
        last.append(aside(near, None, 1, region))
    if first:
        arrive(last_ground)
        prepare(near_ground, radial_in, radial_bias, tiles, places, counts, radial_block)
    for copy in own:
        copy.wait()
    arrive(last)
    for copy in copies:
        copy.wait_send()


def extended(states, dims, identity, extra=()):
    wide, deep, tall = dims
    slots, width = states[0].shape[-2:]
    vmem = pl.BlockSpec(memory_space=pltpu.VMEM)
    anywhere = pl.BlockSpec(memory_space=pl.ANY)
    outer = (tall + 2, deep + 2, wide + 2)
    cells = math.prod(outer)
    shapes = [jax.ShapeDtypeStruct(outer + (4, slots, width), states[0].dtype)]
    out_specs = [anywhere]
    in_specs = [anywhere] * len(states)
    scratch = []
    pieces = 20 + 6 * wide
    if extra:
        layers, basis_count, hidden_width = extra[2].shape
        shapes += [
            jax.ShapeDtypeStruct((cells, slots, 128), jnp.float32),
            jax.ShapeDtypeStruct((1, 128), jnp.int32),
            jax.ShapeDtypeStruct((layers, group * hidden_width, 128), jnp.bfloat16),
        ]
        out_specs += [vmem] * 3
        in_specs = [pl.BlockSpec(memory_space=pltpu.SMEM), vmem] + in_specs + [vmem] * 2
        states = tuple(extra[:2]) + tuple(states) + tuple(extra[2:])
        scratch = [
            pltpu.VMEM(outer + (1, 128), jnp.float32),
            pltpu.VMEM((128, 8, 128), jnp.float32),
        ]
        pieces += 6 + 4 + 2 * wide
    return pl.pallas_call(
        functools.partial(halo_kernel, bool(extra), dims),
        out_shape=shapes,
        in_specs=in_specs,
        out_specs=out_specs,
        scratch_shapes=scratch
        + [
            pltpu.SemaphoreType.DMA((2,)),
            pltpu.SemaphoreType.DMA((pieces,)),
            pltpu.SemaphoreType.DMA((pieces,)),
        ],
        compiler_params=pltpu.CompilerParams(
            collective_id=identity, has_side_effects=True, vmem_limit_bytes=56 << 20
        ),
        name="halo",
    )(*states)


def total_kernel(axes, part, out, held, local_sem, send_sem, recv_sem):
    sizes = [lax.axis_size(axis) for axis in axes]
    partners = []
    for steps in itertools.product(*(range(size) for size in sizes)):
        if any(steps):
            partners.append({axis: beside(axis, step) for axis, step in zip(axes, steps)})
    barrier = pltpu.get_barrier_semaphore()
    for device in partners:
        pl.semaphore_signal(barrier, inc=1, device_id=device, device_id_type=MESH)
    own = pltpu.make_async_copy(part, held.at[pl.ds(0, 1)], local_sem)
    own.start()
    pl.semaphore_wait(barrier, len(partners))
    for place, device in enumerate(partners):
        pltpu.make_async_remote_copy(
            src_ref=part,
            dst_ref=held.at[pl.ds(place + 1, 1)],
            send_sem=send_sem,
            recv_sem=recv_sem,
            device_id=device,
            device_id_type=MESH,
        ).start()
    own.wait()
    rest = held.at[pl.ds(1, len(partners))]
    pltpu.make_async_copy(rest, rest, recv_sem).wait()
    pltpu.make_async_copy(rest, rest, send_sem).wait()
    out[0] = jnp.sum(held[...])


def summed(part, axes, identity):
    count = math.prod(lax.axis_size(axis) for axis in axes)
    vmem = pl.BlockSpec(memory_space=pltpu.VMEM)
    return pl.pallas_call(
        functools.partial(total_kernel, axes),
        out_shape=jax.ShapeDtypeStruct((1,), part.dtype),
        in_specs=[vmem],
        out_specs=pl.BlockSpec(memory_space=pltpu.SMEM),
        scratch_shapes=[
            pltpu.VMEM((count,) + part.shape[1:], part.dtype),
            pltpu.SemaphoreType.DMA,
            pltpu.SemaphoreType.DMA,
            pltpu.SemaphoreType.DMA,
        ],
        compiler_params=pltpu.CompilerParams(
            collective_id=identity, has_side_effects=True, vmem_limit_bytes=56 << 20
        ),
        name="total",
    )(part)


def layer_kernel(dims, basis_count, layer, last, *refs):
    counts, atom_bias_all, readout_in, readout_out = refs[:4]
    fetched = refs[4:10]
    if last:
        scalars_out, vectors_out, part_out = refs[10:13]
    else:
        (block_out,) = refs[10:11]
    places, near, radial_block, radial_out, atom_in, atom_out = refs[-17:-11]
    fresh, near_place, spots, near_state, edges = refs[-11:-6]
    plain_table, turned_table, marks, agenda, slab_sem, fetch_sem = refs[-6:]
    wide, deep, tall = dims
    slots, width = near.shape[4:]
    hidden_width = radial_out.shape[0]

    whole_places, whole_near = fetched[:2]
    fetches = [pltpu.make_async_copy(whole_places, places, fetch_sem.at[0])]
    fetches[0].start()
    slabs = []
    for x in range(wide + 2):
        copy = pltpu.make_async_copy(whole_near.at[:, :, x], near.at[:, :, x], slab_sem.at[x])
        copy.start()
        slabs.append(copy)
    weights = (radial_block, radial_out, atom_in, atom_out)
    for place, (source, target) in enumerate(zip(fetched[2:], weights)):
        copy = pltpu.make_async_copy(source.at[layer], target, fetch_sem.at[place + 1])
        copy.start()
        fetches.append(copy)

    inside = [
        (x, y, z)
        for z in range(1, tall + 1)
        for y in range(1, deep + 1)
        for x in range(1, wide + 1)
    ]
    order = list(itertools.product(range(wide + 2), range(deep + 2), range(tall + 2)))

    def index_of(place):
        x, y, z = place
        return (z * (deep + 2) + y) * (wide + 2) + x

    total = 0
    starts = {}
    bounds = [0]
    fetches[0].wait()
    for place in order:
        starts[place] = total
        near_place[pl.ds(total, slots), :] = places[index_of(place)]
        total = total + counts[0, index_of(place)]
        if place[1:] == (deep + 1, tall + 1):
            bounds.append(total)
    blank = jnp.zeros((table_chunk, width), jnp.float32)
    window = spots.shape[3]
    near_place[pl.ds(total, window), :] = jnp.zeros((window, width), jnp.float32)
    chunks = lax.div(total + table_chunk - 1, table_chunk)
    for number, place in enumerate(inside):
        x = place[0]
        base = lax.div(bounds[x - 1], 16) * 16
        steps = lax.div(bounds[x + 2] - base + chunk - 1, chunk)
        marks[number, 0] = jnp.clip(chunks * table_chunk - steps * chunk, 0, base)
        marks[number, 1] = steps
        marks[number, 2] = starts[place]
        marks[number, 3] = counts[0, index_of(place)]

    for place in order:
        x, y, z = place
        if (y, z) == (0, 0):
            slabs[x].wait()
        for part in range(4):
            near_state[part, pl.ds(starts[place], slots), :] = near[z, y, x, part].astype(
                jnp.float32
            )
    for part in range(4):
        near_state[part, pl.ds(total, table_chunk), :] = blank
    for copy in fetches[1:]:
        copy.wait()

    beyond = pl.ds(pl.multiple_of(chunks * table_chunk, table_chunk), chunk - table_chunk)
    plain_table[beyond, :] = jnp.zeros((chunk - table_chunk, 4 * width), jnp.bfloat16)
    for part in range(3):
        turned_table[part, beyond, :] = jnp.zeros((chunk - table_chunk, 2 * width), jnp.bfloat16)

    @pl.loop(0, chunks)
    def _(step):
        rows = pl.ds(pl.multiple_of(step * table_chunk, table_chunk), table_chunk)
        half = jnp.dot(
            near_state[0, rows, :].astype(jnp.bfloat16),
            (0.5 * atom_in[...].astype(jnp.float32)).astype(jnp.bfloat16),
            preferred_element_type=jnp.float32,
        ) + 0.5 * atom_bias_all[layer : layer + 1, :]
        hidden = (half + half * jnp.tanh(half)).astype(jnp.bfloat16)
        gates = jnp.dot(hidden, atom_out[...], preferred_element_type=jnp.float32).astype(
            jnp.bfloat16
        )
        plain_table[rows, :width] = gates[:, :width]
        gate_b = gates[:, width : 2 * width].astype(jnp.float32)
        gate_c = gates[:, 2 * width : 3 * width]
        gate_g = gates[:, 3 * width :].astype(jnp.float32)
        for part in range(3):
            vector = near_state[part + 1, rows, :]
            plain_table[rows, (part + 1) * width : (part + 2) * width] = (gate_b * vector).astype(
                jnp.bfloat16
            )
            turned_table[part, rows, :width] = gate_c
            turned_table[part, rows, width:] = (gate_g * vector).astype(jnp.bfloat16)

    quarter = math.pi / cutoff
    sharpness = 0.5 * ((basis_count - 1) / cutoff) ** 2
    tile = 16
    fresh[...] = jnp.zeros(fresh.shape, fresh.dtype)

    longest = functools.reduce(jnp.maximum, [marks[number, 1] for number in range(len(inside))])

    @pl.loop(0, longest)
    def _(step):
        columns = pl.ds(pl.multiple_of(step * chunk, chunk), chunk)
        for number in range(len(inside)):
            begin = marks[number, 0] + step * chunk
            start = marks[number, 2]
            line = near_place[pl.ds(begin, chunk), :].T[:8, :]
            mine = near_place[pl.ds(start, slots), :]
            col = begin + lax.broadcasted_iota(jnp.int32, (slots, chunk), 1)
            row = start + lax.broadcasted_iota(jnp.int32, (slots, chunk), 0)
            unused = jnp.logical_or(col == row, col >= total)
            offset = [line[k : k + 1, :] - mine[:, k : k + 1] for k in range(3)]
            square = offset[0] * offset[0] + offset[1] * offset[1] + offset[2] * offset[2]
            square = square + jnp.where(unused, 1.0, 0.0)
            inverse = lax.rsqrt(square)
            distance = square * inverse
            angle = quarter * distance - 0.5 * math.pi
            turn = angle * angle
            series = 0.0
            for power in (13, 11, 9, 7, 5, 3):
                series = turn * (series + (-1.0) ** (power // 2) / math.factorial(power))
            smooth = 0.5 - 0.5 * (angle + angle * series)
            spots[number, 0, :, columns] = distance
            spots[number, 1, :, columns] = jnp.where(
                jnp.logical_and(distance < cutoff, jnp.logical_not(unused)), smooth, 0.0
            )
            for k in range(3):
                spots[number, k + 2, :, columns] = offset[k] * inverse

    tasks = 0
    for number in range(len(inside)):
        steps = marks[number, 1]
        turns = lax.div(marks[number, 3] + group - 1, group)

        @pl.loop(0, turns * steps)
        def _(task, number=number, steps=steps, tasks=tasks):
            turn = lax.div(task, steps)
            agenda[tasks + task, 0] = number
            agenda[tasks + task, 1] = turn * group
            agenda[tasks + task, 2] = task - turn * steps

        tasks = tasks + turns * steps

    share = group // shares

    def spread_basis(task):
        number = agenda[task, 0]
        these = pl.ds(pl.multiple_of(agenda[task, 1], group), group)
        columns = pl.ds(pl.multiple_of(agenda[task, 2] * chunk, chunk), chunk)
        centers = lax.broadcasted_iota(jnp.int32, (1, basis_count, chunk), 1).astype(
            jnp.float32
        ) * (cutoff / (basis_count - 1))
        gap = spots[number, 0, these, columns][:, None, :] - centers
        basis = jnp.exp(-sharpness * gap * gap).reshape(group * basis_count, chunk)
        return jnp.concatenate(
            [basis, jnp.ones((128 - group * basis_count, chunk), jnp.float32)], axis=0
        ).astype(jnp.bfloat16)

    def form_edges(task, basis, part, edges):
        number = agenda[task, 0]
        these = pl.ds(pl.multiple_of(agenda[task, 1], group), group)
        columns = pl.ds(pl.multiple_of(agenda[task, 2] * chunk, chunk), chunk)
        mine = slice(part * share, (part + 1) * share)
        rows = slice(part * share * hidden_width, (part + 1) * share * hidden_width)
        half = jnp.dot(
            radial_block[rows, :], basis, preferred_element_type=jnp.float32
        ).reshape(share, hidden_width, chunk)
        weight = spots[number, 1, these, columns][mine, None, :]
        active = (half + half * jnp.tanh(half)) * weight
        active = active.astype(jnp.bfloat16).reshape(share, hidden_width // tile, tile, chunk)
        edges[0, rows, :] = active.reshape(share * hidden_width, chunk)
        for k in range(3):
            unit = jnp.broadcast_to(
                spots[number, k + 2, these, columns][mine, None, :], (share, tile, chunk)
            ).astype(jnp.bfloat16)
            edges[k + 1, rows, :] = (active * unit[:, None]).reshape(share * hidden_width, chunk)

    def contract(task, edges):
        number = agenda[task, 0]
        these = pl.ds(pl.multiple_of(agenda[task, 1], group), group)
        rows = pl.ds(pl.multiple_of(marks[number, 0] + agenda[task, 2] * chunk, 16), chunk)

        def contracted(left, right, filters):
            product = jnp.dot(left, right, preferred_element_type=jnp.float32)
            product = product.reshape(group, hidden_width, 2 * width)
            return (
                jnp.sum(product[:, :, :width] * filters[0], axis=1),
                jnp.sum(product[:, :, width:] * filters[1], axis=1),
            )

        bank = [
            radial_out[:, part * width : (part + 1) * width].astype(jnp.float32)[None]
            for part in range(4)
        ]
        scalar, vector0 = contracted(edges[0], plain_table[rows, : 2 * width], (bank[0], bank[1]))
        vector1, vector2 = contracted(edges[0], plain_table[rows, 2 * width :], (bank[1], bank[1]))
        vectors = [vector0, vector1, vector2]
        for k in range(3):
            along, project = contracted(edges[k + 1], turned_table[k, rows, :], (bank[2], bank[3]))
            vectors[k] = vectors[k] + along
            scalar = scalar + project
        for part, change in enumerate([scalar] + vectors):
            fresh[number, part, these, :] += change

    @pl.loop(0, tasks)
    def _(task):
        basis = spread_basis(task)
        for part in range(shares):
            form_edges(task, basis, part, edges)
        contract(task, edges)

    energy = jnp.zeros((1, 1), jnp.float32)
    for number, place in enumerate(inside):
        alive = (
            lax.broadcasted_iota(jnp.int32, (slots, width), 0) < counts[0, index_of(place)]
        )
        rounded = [
            jnp.where(
                alive,
                near_state[part, pl.ds(starts[place], slots), :]
                + message_scale * fresh[number, part],
                0.0,
            ).astype(jnp.bfloat16)
            for part in range(4)
        ]
        if last:
            scalars_out[number] = rounded[0]
            for part in range(3):
                vectors_out[number, part] = rounded[part + 1]
            read = lax.dot_general(
                rounded[0],
                readout_in[...],
                (((1,), (1,)), ((), ())),
                preferred_element_type=jnp.float32,
            )
            read = read / (1.0 + jnp.exp(-read)) * readout_out[...]
            read = jnp.where(alive[:, : read.shape[1]], read, 0.0)
            energy = energy + jnp.sum(read, axis=(0, 1), keepdims=True)
        else:
            for part in range(4):
                block_out[number, part] = rounded[part]
    if last:
        spot = lax.broadcasted_iota(jnp.int32, part_out.shape, 1)
        part_out[...] = jnp.where(spot == 0, jnp.broadcast_to(energy, part_out.shape), 0.0)


def layer_update(layer, dims, basis_count, counts, places, near, params):
    wide, deep, tall = dims
    blocks, radial_out, atom_in, atom_bias, atom_out, readout_in, readout_out = params
    around = math.prod(near.shape[:3])
    slots, width = near.shape[4:]
    hidden_width = radial_out.shape[1]
    last = layer == radial_out.shape[0] - 1
    cells = wide * deep * tall
    span = -(-around * slots // table_chunk) * table_chunk + chunk - table_chunk
    window = -(-(3 * (around // (wide + 2)) * slots + 16) // chunk) * chunk
    store = around * slots + window + slots
    vmem = pl.BlockSpec(memory_space=pltpu.VMEM)
    anywhere = pl.BlockSpec(memory_space=pl.ANY)
    if last:
        shapes = (
            jax.ShapeDtypeStruct((cells, slots, width), jnp.bfloat16),
            jax.ShapeDtypeStruct((cells, 3, slots, width), jnp.bfloat16),
            jax.ShapeDtypeStruct((1, 128), jnp.float32),
        )
    else:
        shapes = (jax.ShapeDtypeStruct((cells, 4, slots, width), jnp.bfloat16),)
    fetched = (places, near, blocks, radial_out, atom_in, atom_out)
    return pl.pallas_call(
        functools.partial(layer_kernel, dims, basis_count, layer, last),
        out_shape=shapes,
        in_specs=[pl.BlockSpec(memory_space=pltpu.SMEM)] + [vmem] * 3 + [anywhere] * 6,
        out_specs=tuple(vmem for _ in shapes),
        scratch_shapes=[pltpu.VMEM(array.shape, array.dtype) for array in fetched[:2]]
        + [pltpu.VMEM(array.shape[1:], array.dtype) for array in fetched[2:]]
        + [
            pltpu.VMEM((cells, 4, slots, width), jnp.float32),
            pltpu.VMEM((store, width), jnp.float32),
            pltpu.VMEM((cells, 5, slots, window), jnp.float32),
            pltpu.VMEM((4, store, width), jnp.float32),
            pltpu.VMEM((4, group * hidden_width, chunk), jnp.bfloat16),
            pltpu.VMEM((span, 4 * width), jnp.bfloat16),
            pltpu.VMEM((3, span, 2 * width), jnp.bfloat16),
            pltpu.SMEM((cells, 4), jnp.int32),
            pltpu.SMEM((cells * (slots // group) * (window // chunk), 3), jnp.int32),
            pltpu.SemaphoreType.DMA((wide + 2,)),
            pltpu.SemaphoreType.DMA((5,)),
        ],
        compiler_params=pltpu.CompilerParams(vmem_limit_bytes=56 << 20),
        name="message_layer",
    )(counts, atom_bias, readout_in, readout_out, *fetched)


def on_device(
    positions,
    counts,
    scalars,
    vectors,
    radial_in,
    radial_bias,
    radial_out,
    atom_in,
    atom_bias,
    atom_out,
    readout_in,
    readout_out,
):
    dims = scalars.shape[:3]
    slots, width = scalars.shape[3:]
    level = counts.reshape(-1)
    rows = positions.reshape(-1, 1, slots)
    states = [
        scalars.transpose(2, 1, 0, 3, 4)[:, :, :, None],
        vectors.transpose(2, 1, 0, 4, 3, 5),
    ]
    params = (radial_out, atom_in, atom_bias, atom_out, readout_in.T, readout_out[None, :])
    near, places, near_counts, blocks = extended(
        states, dims, 0, (level, rows, radial_in, radial_bias)
    )
    params = (blocks,) + params
    layers = radial_in.shape[0]
    turned = dims[::-1]
    for layer in range(layers):
        made = layer_update(layer, dims, radial_in.shape[1], near_counts, places, near, params)
        if layer < layers - 1:
            (near,) = extended([made[0].reshape(turned + (4, slots, width))], dims, layer + 1)
    new_scalars, new_vectors, part = made
    scalar_state = new_scalars.reshape(turned + (slots, width)).transpose(2, 1, 0, 3, 4)
    vector_state = new_vectors.reshape(turned + (3, slots, width)).transpose(2, 1, 0, 4, 3, 5)
    energy = summed(part, ("gx", "gy", "gz"), layers)
    return (scalar_state, vector_state, energy)


def solution(mesh):
    block = P("gx", "gy", "gz")
    in_specs = (block,) * 4 + (P(),) * 8
    out_specs = (block, block, P())
    return jax.shard_map(
        on_device, mesh=mesh, in_specs=in_specs, out_specs=out_specs, check_vma=False
    )
```

time: 74.5 us -> 67.2 us (0.902); the launches traced: 73.1 us -> 66.7 us
  Pallas kernels: 68.4 us -> 64.3 us
  other arithmetic: 2 us -> 0 us
    pallas_call x2, Pallas kernels: 42.6 us -> 37.7 us  [extended(): pl.pallas_call(functools.partial(halo_kernel, bool(extra), dims), out_sha...]
    pallas_call x2, Pallas kernels: 12.3 us -> 14.9 us  [layer_update(): pl.pallas_call(functools.partial(layer_kernel, dims, basis_count, layer,...]
    pallas_call x1, Pallas kernels: 13.5 us -> 11.7 us  [summed(): pl.pallas_call(functools.partial(total_kernel, axes), out_shape=jax.Shape...]
where the time goes in v2:
time: 67.2 us; the launch traced here: 66.7 us
  Pallas kernels  64.3 us (96%)
  between operations  2.43 us (4%)
    pallas_call x2, Pallas kernels, extended(): pl.pallas_call(functools.partial(halo_kernel, bool(extra), dims), out_sha...  37.7 us
    pallas_call x2, Pallas kernels, layer_update(): pl.pallas_call(functools.partial(layer_kernel, dims, basis_count, layer,...  14.9 us
    pallas_call x1, Pallas kernels, summed(): pl.pallas_call(functools.partial(total_kernel, axes), out_shape=jax.Shape...  11.7 us

profile of v2, /device:TPU:0, one launch (start us, length us, event | category | flops | bytes accessed | tf_op | source)
XLA Modules:
  0.0 66.7 jit_solution(17510709956040894243)
XLA Ops:
  0.6 19.2 %halo.2 = (bf16[3,3,4,4,32,128]{5,4,3,2,1,0:T(8,128)(2,1)}, f32[36,32,128]{2,1,0:T(8,128)}, s32[1,128]{1,0:T(1,128)}, bf16[2,512,128]{2,1,0:T(8,128)(2,1)}) custom-call(s32[2]{0:T(128)} %bitcast.25, f32[6,1,32]{2,1,0:T(1,128)} %bitcast.22, bf16[1,1,2,1,32,128]{5,4,3,2,1,0:T(8,128)(2,1)} %bitcast.21, bf16[1,1,2,3,32,128]{5,4,3,2,1,0:T(8,128)(2,1)} %bitcast.20, ...), custom_call_target="tpu_custom_call" | custom-call | tf_op jit(solution)/shard_map/halo/pallas_call | solution.py:237
  19.8 7.4 %message_layer.2 = bf16[2,4,32,128]{3,2,1,0:T(8,128)(2,1)} custom-call(s32[1,128]{1,0:T(1,128)} %get-tuple-element.10.refs_0_, f32[2,128]{1,0:T(2,128)} %refs_1_.3, bf16[64,128]{1,0:T(8,128)(2,1)} %bitcast.18, f32[1,64]{1,0:T(1,128)} %bitcast.23, f32[36,32,128]{2,1,0:T(8,128)} %get-tuple-element.11.refs_4_, ...), custom_call_target="tpu_custom_call" | custom-call | tf_op jit(solution)/shard_map/message_layer/pallas_call | solution.py:584
  27.2 18.5 %halo.3.refs_5_ = bf16[3,3,4,4,32,128]{5,4,3,2,1,0:T(8,128)(2,1)} custom-call(bf16[1,1,2,4,32,128]{5,4,3,2,1,0:T(8,128)(2,1)} %bitcast.17), custom_call_target="tpu_custom_call" | custom-call | tf_op jit(solution)/shard_map/halo/pallas_call | solution.py:237
  45.8 7.5 %message_layer.3 = (bf16[2,32,128]{2,1,0:T(8,128)(2,1)}, bf16[2,3,32,128]{3,2,1,0:T(8,128)(2,1)}, f32[1,128]{1,0:T(1,128)}) custom-call(s32[1,128]{1,0:T(1,128)} %get-tuple-element.10.refs_0_, f32[2,128]{1,0:T(2,128)} %refs_1_.3, bf16[64,128]{1,0:T(8,128)(2,1)} %bitcast.19, f32[1,64]{1,0:T(1,128)} %bitcast.24, f32[36,32,128]{2,1,0:T(8,128)} %get-tuple-element.11.refs_4_, ...), custom_call_target="tpu_custom_call" | custom-call | tf_op jit(solution)/shard_map/message_layer/pallas_call | solution.py:584
  53.3 11.7 %total.1 = f32[1]{0:T(128)} custom-call(f32[1,128]{1,0:T(1,128)} %get-tuple-element.16.part), custom_call_target="tpu_custom_call" | custom-call | tf_op jit(solution)/shard_map/total/pallas_call | solution.py:286

commit v3 on v2

--- a/solution.py
+++ b/solution.py
@@ -13,7 +13,7 @@
 message_scale = 0.5
 group = 8
 chunk = 512
-table_chunk = 256
+table_chunk = 512
 shares = 4
 
 MESH = pl.DeviceIdType.MESH
@@ -24,24 +24,20 @@
     return lax.rem(lax.axis_index(axis) + step + count, count)
 
 
-def prepare(near_ground, radial_in, radial_bias, tiles, places, counts, radial_block):
+def prepare(near_ground, radial_in, radial_bias, tiles, counts, radial_block, slots):
     tall, deep, wide = near_ground.shape[:3]
     cells = tall * deep * wide
-    slots = places.shape[1]
     rows = near_ground[...].reshape(cells, 128)
+    cell = lax.broadcasted_iota(jnp.int32, (cells, 128), 0)
+    places = (lax.rem(cell, wide), lax.rem(lax.div(cell, wide), deep), lax.div(cell, wide * deep))
     tiles[...] = jnp.zeros(tiles.shape, tiles.dtype)
-    tiles[:cells, 0, :] = rows
-    for part in range(1, 4):
-        tiles[:cells, part, :] = jnp.concatenate(
-            [rows[:, part * slots :], rows[:, : part * slots]], axis=1
-        )
-    lane = lax.broadcasted_iota(jnp.int32, (slots, 8), 1)
-    for index, (z, y, x) in enumerate(itertools.product(range(tall), range(deep), range(wide))):
-        shift = jnp.where(
-            lane == 0, float(x - 1), jnp.where(lane == 1, float(y - 1), float(z - 1))
-        )
-        places[index, :, :8] = tiles[index].T[:slots, :] + shift * cutoff
-    level = tiles[:, 3, :]
+    for part in range(3):
+        turned = rows
+        if part:
+            turned = jnp.concatenate([rows[:, part * slots :], rows[:, : part * slots]], axis=1)
+        tiles[:, part, :] = turned + (places[part] - 1).astype(jnp.float32) * cutoff
+    level = jnp.concatenate([rows[:, 3 * slots :], rows[:, : 3 * slots]], axis=1)
+    level = jnp.concatenate([level, jnp.zeros((128 - cells, 128), jnp.float32)], axis=0)
     counts[...] = level.T[:1, :].astype(jnp.int32)
 
     layers, basis_count, hidden_width = radial_in.shape
@@ -69,9 +65,12 @@
 def halo_kernel(first, dims, *refs):
     wide, deep, tall = dims
     if first:
-        level, positions, scalars, vectors, radial_in, radial_bias = refs[:6]
-        near, places, counts, radial_block = refs[6:10]
-        near_ground, tiles, own_sem, send_sem, recv_sem = refs[10:]
+        scalars, vectors = refs[2:4]
+        near = refs[6]
+        near_ground = refs[10]
+        level, positions, radial_in, radial_bias = refs[11:15]
+        results = refs[15:18]
+        own_sem, send_sem, recv_sem = refs[18:]
         held = ((scalars, pl.ds(0, 1)), (vectors, pl.ds(1, 3)))
     else:
         block, near, own_sem, send_sem, recv_sem = refs
@@ -92,6 +91,13 @@
         )
         own[-1].start()
     if first:
+        fetches = []
+        sources = refs[:2] + refs[4:6]
+        for place, (source, target) in enumerate(zip(sources, refs[11:15])):
+            fetches.append(pltpu.make_async_copy(source, target, own_sem.at[2 + place]))
+            fetches[-1].start()
+        for copy in fetches:
+            copy.wait()
         slots = positions.shape[-1]
         for z, y, x in itertools.product(range(tall), range(deep), range(wide)):
             at = (x * deep + y) * tall + z
@@ -199,7 +205,10 @@
         last.append(aside(near, None, 1, region))
     if first:
         arrive(last_ground)
-        prepare(near_ground, radial_in, radial_bias, tiles, places, counts, radial_block)
+        prepare(near_ground, radial_in, radial_bias, *results, slots)
+        for place, (source, target) in enumerate(zip(results, refs[7:10])):
+            own.append(pltpu.make_async_copy(source, target, own_sem.at[6 + place]))
+            own[-1].start()
     for copy in own:
         copy.wait()
     arrive(last)
@@ -210,38 +219,33 @@
 def extended(states, dims, identity, extra=()):
     wide, deep, tall = dims
     slots, width = states[0].shape[-2:]
-    vmem = pl.BlockSpec(memory_space=pltpu.VMEM)
     anywhere = pl.BlockSpec(memory_space=pl.ANY)
     outer = (tall + 2, deep + 2, wide + 2)
     cells = math.prod(outer)
     shapes = [jax.ShapeDtypeStruct(outer + (4, slots, width), states[0].dtype)]
-    out_specs = [anywhere]
-    in_specs = [anywhere] * len(states)
     scratch = []
     pieces = 20 + 6 * wide
     if extra:
         layers, basis_count, hidden_width = extra[2].shape
         shapes += [
-            jax.ShapeDtypeStruct((cells, slots, 128), jnp.float32),
+            jax.ShapeDtypeStruct((cells, 8, 128), jnp.float32),
             jax.ShapeDtypeStruct((1, 128), jnp.int32),
             jax.ShapeDtypeStruct((layers, group * hidden_width, 128), jnp.bfloat16),
         ]
-        out_specs += [vmem] * 3
-        in_specs = [pl.BlockSpec(memory_space=pltpu.SMEM), vmem] + in_specs + [vmem] * 2
         states = tuple(extra[:2]) + tuple(states) + tuple(extra[2:])
-        scratch = [
-            pltpu.VMEM(outer + (1, 128), jnp.float32),
-            pltpu.VMEM((128, 8, 128), jnp.float32),
-        ]
+        scratch = [pltpu.VMEM(outer + (1, 128), jnp.float32)]
+        scratch.append(pltpu.SMEM(extra[0].shape, extra[0].dtype))
+        scratch += [pltpu.VMEM(array.shape, array.dtype) for array in extra[1:]]
+        scratch += [pltpu.VMEM(shape.shape, shape.dtype) for shape in shapes[1:]]
         pieces += 6 + 4 + 2 * wide
     return pl.pallas_call(
         functools.partial(halo_kernel, bool(extra), dims),
         out_shape=shapes,
-        in_specs=in_specs,
-        out_specs=out_specs,
+        in_specs=[anywhere] * len(states),
+        out_specs=[anywhere] * len(shapes),
         scratch_shapes=scratch
         + [
-            pltpu.SemaphoreType.DMA((2,)),
+            pltpu.SemaphoreType.DMA((9,)),
             pltpu.SemaphoreType.DMA((pieces,)),
             pltpu.SemaphoreType.DMA((pieces,)),
         ],
@@ -255,7 +259,11 @@
 def total_kernel(axes, part, out, held, local_sem, send_sem, recv_sem):
     sizes = [lax.axis_size(axis) for axis in axes]
     partners = []
-    for steps in itertools.product(*(range(size) for size in sizes)):
+    order = sorted(
+        itertools.product(*(range(size) for size in sizes)),
+        key=lambda steps: -sum(min(step, size - step) for step, size in zip(steps, sizes)),
+    )
+    for steps in order:
         if any(steps):
             partners.append({axis: beside(axis, step) for axis, step in zip(axes, steps)})
     barrier = pltpu.get_barrier_semaphore()
@@ -282,11 +290,10 @@
 
 def summed(part, axes, identity):
     count = math.prod(lax.axis_size(axis) for axis in axes)
-    vmem = pl.BlockSpec(memory_space=pltpu.VMEM)
     return pl.pallas_call(
         functools.partial(total_kernel, axes),
         out_shape=jax.ShapeDtypeStruct((1,), part.dtype),
-        in_specs=[vmem],
+        in_specs=[pl.BlockSpec(memory_space=pl.ANY)],
         out_specs=pl.BlockSpec(memory_space=pltpu.SMEM),
         scratch_shapes=[
             pltpu.VMEM((count,) + part.shape[1:], part.dtype),
@@ -302,30 +309,33 @@
 
 
 def layer_kernel(dims, basis_count, layer, last, *refs):
-    counts, atom_bias_all, readout_in, readout_out = refs[:4]
-    fetched = refs[4:10]
+    fetched = refs[:10]
     if last:
         scalars_out, vectors_out, part_out = refs[10:13]
     else:
         (block_out,) = refs[10:11]
-    places, near, radial_block, radial_out, atom_in, atom_out = refs[-17:-11]
+    counts, tiles, near, radial_block, radial_out, atom_in, atom_out = refs[-21:-14]
+    atom_bias_all, readout_in, readout_out = refs[-14:-11]
     fresh, near_place, spots, near_state, edges = refs[-11:-6]
     plain_table, turned_table, marks, agenda, slab_sem, fetch_sem = refs[-6:]
     wide, deep, tall = dims
     slots, width = near.shape[4:]
     hidden_width = radial_out.shape[0]
 
-    whole_places, whole_near = fetched[:2]
-    fetches = [pltpu.make_async_copy(whole_places, places, fetch_sem.at[0])]
-    fetches[0].start()
-    slabs = []
+    whole_near = fetched[2]
+    slabs, fetches = [], []
+    for place, target in enumerate((counts, tiles)):
+        fetches.append(pltpu.make_async_copy(fetched[place], target, fetch_sem.at[place]))
+        fetches[-1].start()
     for x in range(wide + 2):
         copy = pltpu.make_async_copy(whole_near.at[:, :, x], near.at[:, :, x], slab_sem.at[x])
         copy.start()
         slabs.append(copy)
-    weights = (radial_block, radial_out, atom_in, atom_out)
-    for place, (source, target) in enumerate(zip(fetched[2:], weights)):
-        copy = pltpu.make_async_copy(source.at[layer], target, fetch_sem.at[place + 1])
+    weights = (radial_block, radial_out, atom_in, atom_out, atom_bias_all, readout_in, readout_out)
+    for place, (source, target) in enumerate(zip(fetched[3:], weights)):
+        if place < 4:
+            source = source.at[layer]
+        copy = pltpu.make_async_copy(source, target, fetch_sem.at[place + 2])
         copy.start()
         fetches.append(copy)
 
@@ -344,10 +354,11 @@
     total = 0
     starts = {}
     bounds = [0]
-    fetches[0].wait()
+    for copy in fetches[:2]:
+        copy.wait()
     for place in order:
         starts[place] = total
-        near_place[pl.ds(total, slots), :] = places[index_of(place)]
+        near_place[pl.ds(total, slots), :8] = tiles[index_of(place)].T[:slots, :]
         total = total + counts[0, index_of(place)]
         if place[1:] == (deep + 1, tall + 1):
             bounds.append(total)
@@ -363,48 +374,6 @@
         marks[number, 1] = steps
         marks[number, 2] = starts[place]
         marks[number, 3] = counts[0, index_of(place)]
-
-    for place in order:
-        x, y, z = place
-        if (y, z) == (0, 0):
-            slabs[x].wait()
-        for part in range(4):
-            near_state[part, pl.ds(starts[place], slots), :] = near[z, y, x, part].astype(
-                jnp.float32
-            )
-    for part in range(4):
-        near_state[part, pl.ds(total, table_chunk), :] = blank
-    for copy in fetches[1:]:
-        copy.wait()
-
-    beyond = pl.ds(pl.multiple_of(chunks * table_chunk, table_chunk), chunk - table_chunk)
-    plain_table[beyond, :] = jnp.zeros((chunk - table_chunk, 4 * width), jnp.bfloat16)
-    for part in range(3):
-        turned_table[part, beyond, :] = jnp.zeros((chunk - table_chunk, 2 * width), jnp.bfloat16)
-
-    @pl.loop(0, chunks)
-    def _(step):
-        rows = pl.ds(pl.multiple_of(step * table_chunk, table_chunk), table_chunk)
-        half = jnp.dot(
-            near_state[0, rows, :].astype(jnp.bfloat16),
-            (0.5 * atom_in[...].astype(jnp.float32)).astype(jnp.bfloat16),
-            preferred_element_type=jnp.float32,
-        ) + 0.5 * atom_bias_all[layer : layer + 1, :]
-        hidden = (half + half * jnp.tanh(half)).astype(jnp.bfloat16)
-        gates = jnp.dot(hidden, atom_out[...], preferred_element_type=jnp.float32).astype(
-            jnp.bfloat16
-        )
-        plain_table[rows, :width] = gates[:, :width]
-        gate_b = gates[:, width : 2 * width].astype(jnp.float32)
-        gate_c = gates[:, 2 * width : 3 * width]
-        gate_g = gates[:, 3 * width :].astype(jnp.float32)
-        for part in range(3):
-            vector = near_state[part + 1, rows, :]
-            plain_table[rows, (part + 1) * width : (part + 2) * width] = (gate_b * vector).astype(
-                jnp.bfloat16
-            )
-            turned_table[part, rows, :width] = gate_c
-            turned_table[part, rows, width:] = (gate_g * vector).astype(jnp.bfloat16)
 
     quarter = math.pi / cutoff
     sharpness = 0.5 * ((basis_count - 1) / cutoff) ** 2
@@ -441,6 +410,43 @@
             )
             for k in range(3):
                 spots[number, k + 2, :, columns] = offset[k] * inverse
+
+    for place in order:
+        x, y, z = place
+        if (y, z) == (0, 0):
+            slabs[x].wait()
+        for part in range(4):
+            near_state[part, pl.ds(starts[place], slots), :] = near[z, y, x, part].astype(
+                jnp.float32
+            )
+    for part in range(4):
+        near_state[part, pl.ds(total, table_chunk), :] = blank
+    for copy in fetches[2:]:
+        copy.wait()
+
+    @pl.loop(0, chunks)
+    def _(step):
+        rows = pl.ds(pl.multiple_of(step * table_chunk, table_chunk), table_chunk)
+        half = jnp.dot(
+            near_state[0, rows, :].astype(jnp.bfloat16),
+            (0.5 * atom_in[...].astype(jnp.float32)).astype(jnp.bfloat16),
+            preferred_element_type=jnp.float32,
+        ) + 0.5 * atom_bias_all[layer : layer + 1, :]
+        hidden = (half + half * jnp.tanh(half)).astype(jnp.bfloat16)
+        gates = jnp.dot(hidden, atom_out[...], preferred_element_type=jnp.float32).astype(
+            jnp.bfloat16
+        )
+        plain_table[rows, :width] = gates[:, :width]
+        gate_b = gates[:, width : 2 * width].astype(jnp.float32)
+        gate_c = gates[:, 2 * width : 3 * width]
+        gate_g = gates[:, 3 * width :].astype(jnp.float32)
+        for part in range(3):
+            vector = near_state[part + 1, rows, :]
+            plain_table[rows, (part + 1) * width : (part + 2) * width] = (gate_b * vector).astype(
+                jnp.bfloat16
+            )
+            turned_table[part, rows, :width] = gate_c
+            turned_table[part, rows, width:] = (gate_g * vector).astype(jnp.bfloat16)
 
     tasks = 0
     for number in range(len(inside)):
@@ -559,9 +565,9 @@
         part_out[...] = jnp.where(spot == 0, jnp.broadcast_to(energy, part_out.shape), 0.0)
 
 
-def layer_update(layer, dims, basis_count, counts, places, near, params):
+def layer_update(layer, dims, basis_count, counts, tiles, near, params):
     wide, deep, tall = dims
-    blocks, radial_out, atom_in, atom_bias, atom_out, readout_in, readout_out = params
+    radial_out = params[1]
     around = math.prod(near.shape[:3])
     slots, width = near.shape[4:]
     hidden_width = radial_out.shape[1]
@@ -580,14 +586,16 @@
         )
     else:
         shapes = (jax.ShapeDtypeStruct((cells, 4, slots, width), jnp.bfloat16),)
-    fetched = (places, near, blocks, radial_out, atom_in, atom_out)
+    fetched = (counts, tiles, near) + params
     return pl.pallas_call(
         functools.partial(layer_kernel, dims, basis_count, layer, last),
         out_shape=shapes,
-        in_specs=[pl.BlockSpec(memory_space=pltpu.SMEM)] + [vmem] * 3 + [anywhere] * 6,
+        in_specs=[anywhere] * len(fetched),
         out_specs=tuple(vmem for _ in shapes),
-        scratch_shapes=[pltpu.VMEM(array.shape, array.dtype) for array in fetched[:2]]
-        + [pltpu.VMEM(array.shape[1:], array.dtype) for array in fetched[2:]]
+        scratch_shapes=[pltpu.SMEM(counts.shape, counts.dtype)]
+        + [pltpu.VMEM(array.shape, array.dtype) for array in fetched[1:3]]
+        + [pltpu.VMEM(array.shape[1:], array.dtype) for array in params[:4]]
+        + [pltpu.VMEM(array.shape, array.dtype) for array in params[4:]]
         + [
             pltpu.VMEM((cells, 4, slots, width), jnp.float32),
             pltpu.VMEM((store, width), jnp.float32),
@@ -599,11 +607,11 @@
             pltpu.SMEM((cells, 4), jnp.int32),
             pltpu.SMEM((cells * (slots // group) * (window // chunk), 3), jnp.int32),
             pltpu.SemaphoreType.DMA((wide + 2,)),
-            pltpu.SemaphoreType.DMA((5,)),
+            pltpu.SemaphoreType.DMA((9,)),
         ],
         compiler_params=pltpu.CompilerParams(vmem_limit_bytes=56 << 20),
         name="message_layer",
-    )(counts, atom_bias, readout_in, readout_out, *fetched)
+    )(*fetched)
 
 
 def on_device(
@@ -628,15 +636,15 @@
         scalars.transpose(2, 1, 0, 3, 4)[:, :, :, None],
         vectors.transpose(2, 1, 0, 4, 3, 5),
     ]
-    params = (radial_out, atom_in, atom_bias, atom_out, readout_in.T, readout_out[None, :])
-    near, places, near_counts, blocks = extended(
+    params = (radial_out, atom_in, atom_out, atom_bias, readout_in.T, readout_out[None, :])
+    near, tiles, near_counts, blocks = extended(
         states, dims, 0, (level, rows, radial_in, radial_bias)
     )
     params = (blocks,) + params
     layers = radial_in.shape[0]
     turned = dims[::-1]
     for layer in range(layers):
-        made = layer_update(layer, dims, radial_in.shape[1], near_counts, places, near, params)
+        made = layer_update(layer, dims, radial_in.shape[1], near_counts, tiles, near, params)
         if layer < layers - 1:
             (near,) = extended([made[0].reshape(turned + (4, slots, width))], dims, layer + 1)
     new_scalars, new_vectors, part = made

time: 67.2 us -> 62.5 us (0.930)
  Pallas kernels: 64.3 us -> 60.2 us
    pallas_call x2, Pallas kernels: 14.9 us -> 12.5 us  [layer_update(): pl.pallas_call(functools.partial(layer_kernel, dims, basis_count, layer,...]
    pallas_call x2, Pallas kernels: 37.7 us -> 35.6 us  [extended(): pl.pallas_call(functools.partial(halo_kernel, bool(extra), dims), out_sha...]
where the time goes in v3:
time: 62.5 us; the launch traced here: 62.6 us
  Pallas kernels  60.2 us (96%)
  between operations  2.43 us (4%)
    pallas_call x2, Pallas kernels, extended(): pl.pallas_call(functools.partial(halo_kernel, bool(extra), dims), out_sha...  35.6 us
    pallas_call x2, Pallas kernels, layer_update(): pl.pallas_call(functools.partial(layer_kernel, dims, basis_count, layer,...  12.5 us
    pallas_call x1, Pallas kernels, summed(): pl.pallas_call(functools.partial(total_kernel, axes), out_shape=jax.Shape...  12 us

profile of v3, /device:TPU:0, one launch (start us, length us, event | category | flops | bytes accessed | tf_op | source)
XLA Modules:
  0.0 62.6 jit_solution(921676439260684601)
XLA Ops:
  0.6 17.4 %halo.2 = (bf16[3,3,4,4,32,128]{5,4,3,2,1,0:T(8,128)(2,1)}, f32[36,8,128]{2,1,0:T(8,128)}, s32[1,128]{1,0:T(1,128)}, bf16[2,512,128]{2,1,0:T(8,128)(2,1)}) custom-call(s32[2]{0:T(128)} %bitcast.25, f32[6,1,32]{2,1,0:T(1,128)} %bitcast.22, bf16[1,1,2,1,32,128]{5,4,3,2,1,0:T(8,128)(2,1)} %bitcast.21, bf16[1,1,2,3,32,128]{5,4,3,2,1,0:T(8,128)(2,1)} %bitcast.20, ...), custom_call_target="tpu_custom_call" | custom-call | tf_op jit(solution)/shard_map/halo/pallas_call | solution.py:241
  18.1 6.2 %message_layer.2 = bf16[2,4,32,128]{3,2,1,0:T(8,128)(2,1)} custom-call(s32[1,128]{1,0:T(1,128)} %get-tuple-element.10.refs_0_, f32[36,8,128]{2,1,0:T(8,128)} %get-tuple-element.11.refs_1_, bf16[3,3,4,4,32,128]{5,4,3,2,1,0:T(8,128)(2,1)} %get-tuple-element.12.refs_2_, bf16[2,512,128]{2,1,0:T(8,128)(2,1)} %get-tuple-element.13.refs_3_, ...), custom_call_target="tpu_custom_call" | custom-call | tf_op jit(solution)/shard_map/message_layer/pallas_call | solution.py:590
  24.3 18.2 %halo.3.refs_2_ = bf16[3,3,4,4,32,128]{5,4,3,2,1,0:T(8,128)(2,1)} custom-call(bf16[1,1,2,4,32,128]{5,4,3,2,1,0:T(8,128)(2,1)} %bitcast.17), custom_call_target="tpu_custom_call" | custom-call | tf_op jit(solution)/shard_map/halo/pallas_call | solution.py:241
  42.5 6.3 %message_layer.3 = (bf16[2,32,128]{2,1,0:T(8,128)(2,1)}, bf16[2,3,32,128]{3,2,1,0:T(8,128)(2,1)}, f32[1,128]{1,0:T(1,128)}) custom-call(s32[1,128]{1,0:T(1,128)} %get-tuple-element.10.refs_0_, f32[36,8,128]{2,1,0:T(8,128)} %get-tuple-element.11.refs_1_, bf16[3,3,4,4,32,128]{5,4,3,2,1,0:T(8,128)(2,1)} %halo.3.refs_2_, ...), custom_call_target="tpu_custom_call" | custom-call | tf_op jit(solution)/shard_map/message_layer/pallas_call | solution.py:590
  48.8 12.0 %total.1 = f32[1]{0:T(128)} custom-call(f32[1,128]{1,0:T(1,128)} %get-tuple-element.16.part), custom_call_target="tpu_custom_call" | custom-call | tf_op jit(solution)/shard_map/total/pallas_call | solution.py:293

commit v4 on v3

--- a/solution.py
+++ b/solution.py
@@ -173,8 +173,7 @@
         ground_y = both(near_ground, None, "gy", own_part)
     for x, step in sides:
         along_y[x, step] = begin("gy", step, send, {**own_part, "gx": pl.ds(x, 1)})
-    for step in (-1, 1):
-        last += begin("gz", step, sideways, own_part)
+    last += begin("gz", -1, sideways, own_part)
     for step in (-1, 1):
         along_x[step] = begin("gx", step, send, own_part)
     if first:
@@ -182,15 +181,16 @@
         ground_x = both(near_ground, None, "gx", {**own_part, "gy": every["gy"]})
     for step in (-1, 1):
         arrive(along_x[step])
-        region = {**own_part, "gx": edge["gx"][step]}
-        last += [aside(near, None, -1, region), aside(near, None, 1, region)]
-    crossed, turned = {}, []
+        last.append(aside(near, None, -1, {**own_part, "gx": edge["gx"][step]}))
+    for copy in own:
+        copy.wait()
+    last.append(aside(near, None, 1, {**own_part, "gx": every["gx"]}))
+    crossed, turned = {}, {-1: [], 1: []}
     for x, step in sides:
         arrive(along_y[x, step])
         region = {**own_part, "gy": edge["gy"][step], "gx": pl.ds(x, 1)}
         crossed[x, step] = aside(near, None, -1, region)
-        turned += [(step, *sent) for sent in outward(x, region)]
-        last.append(aside(near, None, 1, region))
+        turned[step] += [copy for _, copy in outward(x, region)]
     if first:
         arrive(ground_x)
         last_ground = both(near_ground, None, "gz", {**every})
@@ -199,18 +199,19 @@
         arrive([copy])
         region = {"gy": edge["gy"][step], "gx": pl.ds(x, 1), "gz": far}
         last += [copy for _, copy in outward(x, region)]
-    for step, step_x, copy in turned:
-        arrive([copy])
-        region = {**own_part, "gy": edge["gy"][step], "gx": edge["gx"][step_x]}
+    for step in (-1, 1):
+        arrive(turned[step])
+        region = {**own_part, "gy": edge["gy"][step], "gx": every["gx"]}
         last.append(aside(near, None, 1, region))
     if first:
         arrive(last_ground)
         prepare(near_ground, radial_in, radial_bias, *results, slots)
+        made = []
         for place, (source, target) in enumerate(zip(results, refs[7:10])):
-            own.append(pltpu.make_async_copy(source, target, own_sem.at[6 + place]))
-            own[-1].start()
-    for copy in own:
-        copy.wait()
+            made.append(pltpu.make_async_copy(source, target, own_sem.at[6 + place]))
+            made[-1].start()
+        for copy in made:
+            copy.wait()
     arrive(last)
     for copy in copies:
         copy.wait_send()
@@ -224,7 +225,7 @@
     cells = math.prod(outer)
     shapes = [jax.ShapeDtypeStruct(outer + (4, slots, width), states[0].dtype)]
     scratch = []
-    pieces = 20 + 6 * wide
+    pieces = 16 + 4 * wide
     if extra:
         layers, basis_count, hidden_width = extra[2].shape
         shapes += [
@@ -237,7 +238,7 @@
         scratch.append(pltpu.SMEM(extra[0].shape, extra[0].dtype))
         scratch += [pltpu.VMEM(array.shape, array.dtype) for array in extra[1:]]
         scratch += [pltpu.VMEM(shape.shape, shape.dtype) for shape in shapes[1:]]
-        pieces += 6 + 4 + 2 * wide
+        pieces += 6 + 3 + 2 * wide
     return pl.pallas_call(
         functools.partial(halo_kernel, bool(extra), dims),
         out_shape=shapes,

time: 62.5 us -> 62.6 us (level)
  no operation moved by 1% of the time
where the time goes in v4:
time: 62.6 us; the launch traced here: 63.1 us
  Pallas kernels  60.7 us (97%)
  between operations  2.43 us (4%)
    pallas_call x2, Pallas kernels, extended(): pl.pallas_call(functools.partial(halo_kernel, bool(extra), dims), out_sha...  36 us
    pallas_call x2, Pallas kernels, layer_update(): pl.pallas_call(functools.partial(layer_kernel, dims, basis_count, layer,...  12.5 us
    pallas_call x1, Pallas kernels, summed(): pl.pallas_call(functools.partial(total_kernel, axes), out_shape=jax.Shape...  12.1 us

profile of v4, /device:TPU:0, one launch (start us, length us, event | category | flops | bytes accessed | tf_op | source)
XLA Modules:
  0.0 63.1 jit_solution(7989272162070995974)
XLA Ops:
  0.6 17.2 %halo.2 = (bf16[3,3,4,4,32,128]{5,4,3,2,1,0:T(8,128)(2,1)}, f32[36,8,128]{2,1,0:T(8,128)}, s32[1,128]{1,0:T(1,128)}, bf16[2,512,128]{2,1,0:T(8,128)(2,1)}) custom-call(s32[2]{0:T(128)} %bitcast.25, f32[6,1,32]{2,1,0:T(1,128)} %bitcast.22, bf16[1,1,2,1,32,128]{5,4,3,2,1,0:T(8,128)(2,1)} %bitcast.21, bf16[1,1,2,3,32,128]{5,4,3,2,1,0:T(8,128)(2,1)} %bitcast.20, ...), custom_call_target="tpu_custom_call" | custom-call | tf_op jit(solution)/shard_map/halo/pallas_call | solution.py:242
  17.9 6.2 %message_layer.2 = bf16[2,4,32,128]{3,2,1,0:T(8,128)(2,1)} custom-call(s32[1,128]{1,0:T(1,128)} %get-tuple-element.10.refs_0_, f32[36,8,128]{2,1,0:T(8,128)} %get-tuple-element.11.refs_1_, bf16[3,3,4,4,32,128]{5,4,3,2,1,0:T(8,128)(2,1)} %get-tuple-element.12.refs_2_, bf16[2,512,128]{2,1,0:T(8,128)(2,1)} %get-tuple-element.13.refs_3_, ...), custom_call_target="tpu_custom_call" | custom-call | tf_op jit(solution)/shard_map/message_layer/pallas_call | solution.py:591
  24.1 18.8 %halo.3.refs_2_ = bf16[3,3,4,4,32,128]{5,4,3,2,1,0:T(8,128)(2,1)} custom-call(bf16[1,1,2,4,32,128]{5,4,3,2,1,0:T(8,128)(2,1)} %bitcast.17), custom_call_target="tpu_custom_call" | custom-call | tf_op jit(solution)/shard_map/halo/pallas_call | solution.py:242
  42.9 6.3 %message_layer.3 = (bf16[2,32,128]{2,1,0:T(8,128)(2,1)}, bf16[2,3,32,128]{3,2,1,0:T(8,128)(2,1)}, f32[1,128]{1,0:T(1,128)}) custom-call(s32[1,128]{1,0:T(1,128)} %get-tuple-element.10.refs_0_, f32[36,8,128]{2,1,0:T(8,128)} %get-tuple-element.11.refs_1_, bf16[3,3,4,4,32,128]{5,4,3,2,1,0:T(8,128)(2,1)} %halo.3.refs_2_, ...), custom_call_target="tpu_custom_call" | custom-call | tf_op jit(solution)/shard_map/message_layer/pallas_call | solution.py:591
  49.2 12.1 %total.1 = f32[1]{0:T(128)} custom-call(f32[1,128]{1,0:T(1,128)} %get-tuple-element.16.part), custom_call_target="tpu_custom_call" | custom-call | tf_op jit(solution)/shard_map/total/pallas_call | solution.py:294

commit v5 on v4

--- a/solution.py
+++ b/solution.py
@@ -488,8 +488,10 @@
             radial_block[rows, :], basis, preferred_element_type=jnp.float32
         ).reshape(share, hidden_width, chunk)
         weight = spots[number, 1, these, columns][mine, None, :]
-        active = (half + half * jnp.tanh(half)) * weight
-        active = active.astype(jnp.bfloat16).reshape(share, hidden_width // tile, tile, chunk)
+        active = (half + half * jnp.tanh(half)).astype(jnp.bfloat16)
+        active = active.reshape(share, hidden_width // tile, tile, chunk)
+        weight = jnp.broadcast_to(weight, (share, tile, chunk)).astype(jnp.bfloat16)
+        active = active * weight[:, None]
         edges[0, rows, :] = active.reshape(share * hidden_width, chunk)
         for k in range(3):
             unit = jnp.broadcast_to(

time: 62.6 us -> 62.7 us (level); the launches traced: 63.1 us -> 62 us
  Pallas kernels: 60.7 us -> 59.6 us
    pallas_call x2, Pallas kernels: 12.5 us -> 10.3 us  [layer_update(): pl.pallas_call(functools.partial(layer_kernel, dims, basis_count, layer,...]
    pallas_call x2, Pallas kernels: 36 us -> 36.8 us  [extended(): pl.pallas_call(functools.partial(halo_kernel, bool(extra), dims), out_sha...]
where the time goes in v5:
time: 62.7 us; the launch traced here: 62 us
  Pallas kernels  59.6 us (95%)
  between operations  2.43 us (4%)
    pallas_call x2, Pallas kernels, extended(): pl.pallas_call(functools.partial(halo_kernel, bool(extra), dims), out_sha...  36.8 us
    pallas_call x1, Pallas kernels, summed(): pl.pallas_call(functools.partial(total_kernel, axes), out_shape=jax.Shape...  12.4 us
    pallas_call x2, Pallas kernels, layer_update(): pl.pallas_call(functools.partial(layer_kernel, dims, basis_count, layer,...  10.3 us

profile of v5, /device:TPU:0, one launch (start us, length us, event | category | flops | bytes accessed | tf_op | source)
XLA Modules:
  0.0 62.0 jit_solution(15190098574837205305)
XLA Ops:
  0.6 17.2 %halo.2 = (bf16[3,3,4,4,32,128]{5,4,3,2,1,0:T(8,128)(2,1)}, f32[36,8,128]{2,1,0:T(8,128)}, s32[1,128]{1,0:T(1,128)}, bf16[2,512,128]{2,1,0:T(8,128)(2,1)}) custom-call(s32[2]{0:T(128)} %bitcast.25, f32[6,1,32]{2,1,0:T(1,128)} %bitcast.22, bf16[1,1,2,1,32,128]{5,4,3,2,1,0:T(8,128)(2,1)} %bitcast.21, bf16[1,1,2,3,32,128]{5,4,3,2,1,0:T(8,128)(2,1)} %bitcast.20, ...), custom_call_target="tpu_custom_call" | custom-call | tf_op jit(solution)/shard_map/halo/pallas_call | solution.py:242
  17.9 5.1 %message_layer.2 = bf16[2,4,32,128]{3,2,1,0:T(8,128)(2,1)} custom-call(s32[1,128]{1,0:T(1,128)} %get-tuple-element.10.refs_0_, f32[36,8,128]{2,1,0:T(8,128)} %get-tuple-element.11.refs_1_, bf16[3,3,4,4,32,128]{5,4,3,2,1,0:T(8,128)(2,1)} %get-tuple-element.12.refs_2_, bf16[2,512,128]{2,1,0:T(8,128)(2,1)} %get-tuple-element.13.refs_3_, ...), custom_call_target="tpu_custom_call" | custom-call | tf_op jit(solution)/shard_map/message_layer/pallas_call | solution.py:593
  23.0 19.6 %halo.3.refs_2_ = bf16[3,3,4,4,32,128]{5,4,3,2,1,0:T(8,128)(2,1)} custom-call(bf16[1,1,2,4,32,128]{5,4,3,2,1,0:T(8,128)(2,1)} %bitcast.17), custom_call_target="tpu_custom_call" | custom-call | tf_op jit(solution)/shard_map/halo/pallas_call | solution.py:242
  42.6 5.2 %message_layer.3 = (bf16[2,32,128]{2,1,0:T(8,128)(2,1)}, bf16[2,3,32,128]{3,2,1,0:T(8,128)(2,1)}, f32[1,128]{1,0:T(1,128)}) custom-call(s32[1,128]{1,0:T(1,128)} %get-tuple-element.10.refs_0_, f32[36,8,128]{2,1,0:T(8,128)} %get-tuple-element.11.refs_1_, bf16[3,3,4,4,32,128]{5,4,3,2,1,0:T(8,128)(2,1)} %halo.3.refs_2_, ...), custom_call_target="tpu_custom_call" | custom-call | tf_op jit(solution)/shard_map/message_layer/pallas_call | solution.py:593
  47.8 12.4 %total.1 = f32[1]{0:T(128)} custom-call(f32[1,128]{1,0:T(1,128)} %get-tuple-element.16.part), custom_call_target="tpu_custom_call" | custom-call | tf_op jit(solution)/shard_map/total/pallas_call | solution.py:294
